TPU v7x, 32 devices: a whole 2x2x4 slice. The times are simulated.
32 devices in a mesh: shot: 4 (over x, core), band: 4 (over z), net: 2 (over y).
Axes of the slice: x: 2, y: 2, z: 4, core: 2. Of those that a mesh axis runs over, the one named last changes fastest.
Arguments:
- velocity: float32 [128, 1024], P('band'), may hold values from 1.5 to 4
- wave_now: float32 [16, 128, 1024], P(('shot', 'net'), 'band'), may hold values from -6 to 6
- wave_before: float32 [16, 128, 1024], P(('shot', 'net'), 'band'), may hold values from -6 to 6
- adjoint_last: float32 [16, 128, 1024], P(('shot', 'net'), 'band'), may hold values from -6 to 6
- adjoint_after: float32 [16, 128, 1024], P(('shot', 'net'), 'band'), may hold values from -6 to 6
- wavelet: float32 [16, 16], P(('shot', 'net')), may hold values from -72 to 72
- source_col: int32 [16], P(('shot', 'net')), may hold values from 0 to 1023
- rec_first: int32 [16], P(('shot', 'net')), may hold values from 0 to 1022
- rec_last: int32 [16], P(('shot', 'net')), may hold values from 1 to 1023
- rec_count: int32 [16], P(('shot', 'net')), may hold values from 2 to 128, as said below
- observed: float32 [16, 16, 128], P(('shot', 'net')), may hold values from -72 to 72
- conv_in: float32 [32, 18], replicated, may hold values from -1.5 to 1.5
- conv_mid: float32 [32, 288], replicated, may hold values from -0.375 to 0.375
- conv_out: float32 [1, 288], replicated, may hold values from -0.375 to 0.375
- cotangent: float32 [128, 1024], P('band', ('shot', 'net')), may hold values from -0.06629126 to 0.06629126
Outputs:
- new_velocity: float32 [128, 1024], P('band', ('shot', 'net'))
- grad_in: float32 [32, 18], replicated
- grad_mid: float32 [32, 288], replicated
- grad_out: float32 [1, 288], replicated
Inputs may be any that keep to these rules, and one draw needn't show every extreme that they name: rec_last - rec_first >= rec_count - 1 for every shot; some shot has 128 receivers.
All inputs are finite; a program needn't handle non-finite values.
Results may differ from a plain program's by a relative error of at most 0.0003.
Values sent between devices are 32-bit elements; how exact they have to be, the bound alone decides.
A program may use at most 128 MiB of HBM per device.

v0:
```python
import jax
import jax.numpy as jnp
from jax import lax
from jax.sharding import PartitionSpec as P

coefficients = (-205.0 / 72.0, 8.0 / 5.0, -1.0 / 5.0, 8.0 / 315.0, -1.0 / 560.0)
speed_factor = 0.11
source_depth = 2
receiver_depth = 3
highest = lax.Precision.HIGHEST


def extended_2(block, sides, width):
    for axis, dim in sides:
        count = lax.axis_size(axis)
        forward = [(i, i + 1) for i in range(count - 1)]
        backward = [(target, source) for source, target in forward]
        low = lax.ppermute(
            lax.slice_in_dim(block, block.shape[dim] - width, None, axis=dim), axis, forward
        )
        high = lax.ppermute(lax.slice_in_dim(block, 0, width, axis=dim), axis, backward)
        block = jnp.concatenate([low, block, high], axis=dim)
    return block


def laplace(extended):
    middle = extended[..., 4:-4, :]
    height = middle.shape[-2]
    breadth = middle.shape[-1]
    padding = [(0, 0)] * (middle.ndim - 1) + [(4, 4)]
    padded = jnp.pad(middle, padding)
    running = 2.0 * coefficients[0] * middle
    for reach in range(1, 5):
        vertical = (
            extended[..., 4 - reach : 4 - reach + height, :]
            + extended[..., 4 + reach : 4 + reach + height, :]
        )
        lateral = (
            padded[..., 4 - reach : 4 - reach + breadth]
            + padded[..., 4 + reach : 4 + reach + breadth]
        )
        running = running + coefficients[reach] * (vertical + lateral)
    return running


def receiver_table(rec_first, rec_last, rec_count, breadth, slots):
    columns = jnp.arange(breadth, dtype=jnp.int32)
    slot_ids = jnp.arange(slots, dtype=jnp.int32)
    placed = (
        rec_first[:, None]
        + slot_ids[None, :] * (rec_last - rec_first)[:, None] // (rec_count - 1)[:, None]
    )
    active = slot_ids[None, :] < rec_count[:, None]
    return ((columns[None, :, None] == placed[:, None, :]) & active[:, None, :]).astype(jnp.float32)


def patches(extended, height, breadth):
    parts = [
        extended[:, down : down + height, across : across + breadth]
        for down in range(3)
        for across in range(3)
    ]
    return jnp.concatenate(parts, 0).reshape(-1, height * breadth)


def flipped(weights):
    outputs = weights.shape[0]
    channels = weights.shape[1] // 9
    return (
        weights.reshape(outputs, 9, channels)[:, ::-1, :]
        .transpose(2, 1, 0)
        .reshape(channels, 9 * outputs)
    )


def sigmoid_slope(values):
    squashed = jax.nn.sigmoid(values)
    return squashed * (1.0 + values * (1.0 - squashed))


def matmul(left, right):
    return jnp.dot(left, right, precision=highest)


def outer_sum(left, right):
    return lax.dot_general(left, right, (((1,), (1,)), ((), ())), precision=highest)


def on_device(
    velocity,
    wave_now,
    wave_before,
    adjoint_last,
    adjoint_after,
    wavelet,
    source_col,
    rec_first,
    rec_last,
    rec_count,
    observed,
    conv_in,
    conv_mid,
    conv_out,
    cotangent,
):
    rows_here = velocity.shape[0]
    breadth = velocity.shape[1]
    shot_here = wave_now.shape[0]
    num_steps = wavelet.shape[1]
    slots = observed.shape[2]
    piece_cols = cotangent.shape[1]
    first_row = lax.axis_index("band") * rows_here
    speed_sq = (velocity * speed_factor) ** 2
    columns = jnp.arange(breadth, dtype=jnp.int32)
    source_cols = (columns[None, :] == source_col[:, None]).astype(jnp.float32)[:, None, :]
    table = receiver_table(rec_first, rec_last, rec_count, breadth, slots)
    active = (jnp.arange(slots, dtype=jnp.int32)[None, :] < rec_count[:, None]).astype(jnp.float32)

    def source_term(row_start, height, amount):
        row_ids = row_start + jnp.arange(height, dtype=jnp.int32)
        marked = (row_ids == source_depth).astype(jnp.float32)[None, :, None]
        return marked * source_cols * amount[:, None, None]

    def receiver_term(row_start, height, residual):
        row_ids = row_start + jnp.arange(height, dtype=jnp.int32)
        marked = (row_ids == receiver_depth).astype(jnp.float32)[None, :, None]
        injected = jnp.einsum("swk,sk->sw", table, residual, precision=highest)
        return marked * injected[:, None, :]

    speed_wide = extended_2(speed_sq, (("band", 0),), 16)

    def propagate(start, prior, drive, inject):
        grouped = drive.reshape((num_steps // 4, 4) + drive.shape[1:])

        def block(carry, amounts):
            stacked = extended_2(jnp.stack([carry[0], carry[1]]), (("band", 2),), 16)
            current = stacked[0]
            earlier = stacked[1]
            margin = 16
            saved = []
            for offset in range(4):
                inner = margin - 4
                speed_part = speed_wide[16 - inner : 16 + rows_here + inner]
                fresh = (
                    2.0 * current[:, 4:-4]
                    - earlier[:, 4:-4]
                    + speed_part * laplace(current)
                    + inject(first_row - inner, rows_here + 2 * inner, amounts[offset])
                )
                earlier = current[:, 4:-4]
                current = fresh
                margin = inner
                saved.append(fresh[:, inner : inner + rows_here])
            return ((current, earlier), jnp.stack(saved))

        ignored, states = lax.scan(block, (start, prior), grouped)
        return states.reshape((num_steps,) + start.shape)

    stored = propagate(wave_now, wave_before, wavelet.T, source_term)
    samples = jnp.einsum("tsw,swk->tsk", stored[:, :, receiver_depth, :], table, precision=highest)
    misfit = (samples - jnp.transpose(observed, (1, 0, 2))) * active[None]
    adjoint = propagate(adjoint_last, adjoint_after, misfit[::-1], receiver_term)
    imaging = jnp.sum(stored * adjoint[::-1], axis=(0, 1))
    group_count = shot_here * lax.axis_size(("shot", "net"))
    start_col = lax.axis_index(("shot", "net")) * piece_cols
    gathered = lax.psum(imaging, ("shot", "net"))
    summed = lax.dynamic_slice_in_dim(gathered, start_col, piece_cols, 1)
    scaled = summed / float(num_steps * group_count) ** 0.5
    velocity_piece = lax.dynamic_slice_in_dim(velocity, start_col, piece_cols, 1)

    def spread(field):
        extended = extended_2(field, (("band", 1), (("shot", "net"), 2)), 1)
        return patches(extended, rows_here, piece_cols)

    layer_zero = spread(jnp.stack([velocity_piece, scaled]))
    before_one = matmul(conv_in, layer_zero)
    hidden_one = jax.nn.silu(before_one)
    layer_one = spread(hidden_one.reshape(-1, rows_here, piece_cols))
    before_two = matmul(conv_mid, layer_one)
    hidden_two = jax.nn.silu(before_two)
    layer_two = spread(hidden_two.reshape(-1, rows_here, piece_cols))
    update = matmul(conv_out, layer_two).reshape(rows_here, piece_cols)
    new_velocity = velocity_piece + update
    grad_out = outer_sum(cotangent.reshape(1, -1), layer_two)
    slope_two = matmul(flipped(conv_out), spread(cotangent[None])) * sigmoid_slope(before_two)
    grad_mid = outer_sum(slope_two, layer_one)
    slope_one = matmul(
        flipped(conv_mid), spread(slope_two.reshape(-1, rows_here, piece_cols))
    ) * sigmoid_slope(before_one)
    grad_in = outer_sum(slope_one, layer_zero)
    totals = lax.psum((grad_in, grad_mid, grad_out), ("shot", "band", "net"))
    return (new_velocity, totals[0], totals[1], totals[2])


def solution(mesh):
    in_specs = (
        P("band", None),
        P(("shot", "net"), "band", None),
        P(("shot", "net"), "band", None),
        P(("shot", "net"), "band", None),
        P(("shot", "net"), "band", None),
        P(("shot", "net"), None),
        P(("shot", "net")),
        P(("shot", "net")),
        P(("shot", "net")),
        P(("shot", "net")),
        P(("shot", "net"), None, None),
        P(),
        P(),
        P(),
        P("band", ("shot", "net")),
    )
    out_specs = (P("band", ("shot", "net")), P(), P(), P())
    return jax.shard_map(
        on_device, mesh=mesh, in_specs=in_specs, out_specs=out_specs, check_vma=False
    )
```

profile of v0, /device:TPU:0, one launch (start us, length us, event | category | flops | bytes accessed | tf_op | source)
XLA Modules:
  0.0 534.2 jit_solution(12603834938900833449)
XLA Ops:
  8.0 4.9 collective-permute-start.18
  15.2 4.5 collective-permute-start.4
  31.4 4.5 collective-permute-start.20
  40.0 62.5 %while.34 = (s32[]{:T(128)}, f32[2,32,1024]{2,1,0:T(8,128)S(1)}, f32[2,32,1024]{2,1,0:T(8,128)S(1)}, f32[4,4,2,32,1024]{4,3,2,1,0:T(8,128)}, f32[64,1024]{1,0:T(...) while((s32[]{:T(128)}, f32[2,32,1024]{2,1,0:T(8,128)S(1)}, ...), condition=%wide.region_1.2_spmd.clone, body=%wide.region_0.1_spmd.clone.sunk | while | flops 11801106 | bytes 31434516 | solution.py:156
  41.3 5.2 collective-permute-start.1
  46.7 3.9 collective-permute-done
  58.0 5.0 collective-permute-start.1
  63.3 3.0 collective-permute-done
  73.7 5.0 collective-permute-start.1
  88.8 5.0 collective-permute-start.1
  102.5 4.6 copy.175
  110.2 61.3 %while.35 = (s32[]{:T(128)}, f32[2,32,1024]{2,1,0:T(8,128)S(1)}, f32[2,32,1024]{2,1,0:T(8,128)S(1)}, f32[4,4,2,32,1024]{4,3,2,1,0:T(8,128)}, f32[64,1024]{1,0:T(...) while((s32[]{:T(128)}, f32[2,32,1024]{2,1,0:T(8,128)S(1)}, ...), condition=%wide.region_3.4_spmd.clone, body=%wide.region_2.3_spmd.clone.sunk | while | flops 27165204 | bytes 31534800 | solution.py:156
  111.7 5.0 collective-permute-start.3
  127.3 4.6 collective-permute-start.3
  142.5 4.6 collective-permute-start.3
  157.7 4.6 collective-permute-start.3
  171.5 6.6 %copy.176 = f32[16,2,32,1024]{3,0,1,2:T(8,128)} copy(f32[16,2,32,1024]{3,2,1,0:T(8,128)} %bitcast.368) | data formatting | bytes 8388608 | tf_op jit(solution)/shard_map/reshape | solution.py:157
  178.1 6.9 %rev.13 = f32[16,2,32,1024]{3,0,1,2:T(8,128)} reverse(f32[16,2,32,1024]{3,0,1,2:T(8,128)} %copy.176), dimensions={0} | reverse | bytes 8388608 | tf_op jit(solution)/shard_map/rev | solution.py:163
  185.0 7.0 %multiply_reduce_fusion = f32[32,1024]{1,0:T(8,128)} fusion(f32[16,2,32,1024]{3,0,1,2:T(8,128)} %rev.13, f32[16,2,32,1024]{3,2,1,0:T(8,128)} %bitcast.367), kind=kLoop, calls=%fused_computation.332 | loop fusion | flops 2064384 | bytes 8519680 | tf_op jit(solution)/shard_map/reduce_sum | solution.py:163
  192.2 55.1 %all-reduce.11.cloned.1.call-done = f32[32,1024]{1,0:T(8,128)} async-done(((f32[32,1024]{1,0:T(8,128)}), f32[32,1024]{1,0:T(8,128)}) %all-reduce.11.cloned.1.call-update) | async-done | bytes 131088 | tf_op jit(solution)/shard_map/psum | solution.py:166
  248.0 3.4 collective-permute-start.6
  253.4 3.4 collective-permute-done.7
  258.3 4.5 collective-permute-start.8
  268.0 5.1 collective-permute-start.10
  276.6 3.6 copy.125
  280.2 2.9 copy.127
  285.5 5.3 collective-permute-start.12
  292.8 4.4 pad_maximum_fusion.4
  297.3 3.7 fusion.218
  301.0 3.5 copy.135
  304.5 3.5 copy.132
  307.9 3.4 copy.130
  311.4 3.8 fusion.219
  315.2 3.6 copy.133
  318.8 3.4 copy.131
  332.5 3.2 convolution_bitcast_fusion.2
  336.6 4.7 fusion.230
  344.2 5.1 collective-permute-start.14
  357.0 5.1 collective-permute-start.22
  362.1 3.6 copy.138
  365.7 2.9 copy.140
  371.5 5.1 collective-permute-start.16
  376.6 3.6 copy.151
  380.2 3.6 copy.153
  386.3 5.0 collective-permute-start.24
  395.0 3.6 pad_maximum_fusion.6
  398.5 3.2 fusion.214
  401.8 3.4 copy.161
  405.2 3.5 copy.158
  410.8 7.1 %pad_maximum_fusion.5 = (f32[32,34,129]{1,0,2:T(8,128)S(1)}, f32[32,34,129]{1,0,2:T(8,128)S(1)}) fusion(f32[32,34,1]{1,0,2:T(8,128)} %collective-permute-done.17, f32[32,1,128]{1,0,2:T(8,128)} %copy.140, f32[32,32,128]{1,0,2:T(8,128)} %copy-done.6, f32[32,1,128]{1,0,2:T(8,128)} %copy.138, f32[32,34,1]{1,0,2:T(8,128)} %collective-permute-done.16), kind=kLoop, calls=%fused_computation.336 | loop fusion | flops 842112 | bytes 1688576 | tf_op jit(solution)/shard_map/concatenate | solution.py:22
  417.9 3.9 fusion.216
  421.8 3.5 copy.148
  425.2 3.6 copy.145
  428.9 3.5 copy.143
  432.3 6.7 %fusion.215 = (f32[32,32,128]{1,0,2:T(8,128)}, f32[32,32,128]{1,0,2:T(8,128)}, f32[32,32,128]{1,0,2:T(8,128)}) fusion(f32[32,34,129]{1,0,2:T(8,128)} %get-tuple-element.522), kind=kLoop, calls=%fused_computation.439 | loop fusion | bytes 3145728 | tf_op jit(solution)/shard_map/slice | solution.py:59
  439.1 3.5 copy.159
  442.5 3.5 copy.157
  446.1 3.5 copy.154
  456.5 3.2 fusion.193
  461.1 3.8 fusion.217
  464.9 3.6 copy.146
  468.5 3.5 copy.144
  482.8 3.8 fusion.231
  487.9 39.2 %all-reduce.8 = (f32[32,18]{0,1:T(8,128)}, f32[32,288]{1,0:T(8,128)}, f32[1,288]{1,0:T(1,128)}) all-reduce(f32[32,18]{0,1:T(8,128)S(1)} %copy-done.41, f32[32,288]{1,0:T(8,128)S(1)} %copy-done.38, f32[1,288]{1,0:T(1,128)S(1)} %fusion.231), channel_id=1, replica_groups=mesh['shot'=4,'band'=4,'net'=2] {'shot','band','net'}, use_global_device_ids=true, to_apply=%region_6.7 | all-reduce | flops 10080 | bytes 80640 | tf_op jit(solution)/shard_map/psum | solution.py:191
  (455 shorter events, 167.9 us)
Async XLA Ops:
  7.2 258.0 %copy-start = (f32[32,18]{0,1:T(8,128)S(1)}, f32[32,18]{0,1:T(8,128)}, u32[]{:S(2)}) copy-start(f32[32,18]{0,1:T(8,128)} %param.30) | copy-start | bytes 6916
  7.2 32.8 %copy-start.3 = (f32[2,32,1024]{2,1,0:T(8,128)S(1)}, f32[2,32,1024]{2,1,0:T(8,128)}, u32[]{:S(2)}) copy-start(f32[2,32,1024]{2,1,0:T(8,128)} %param.20) | copy-start | bytes 786436
  7.2 32.8 %copy-start.4 = (f32[2,32,1024]{2,1,0:T(8,128)S(1)}, f32[2,32,1024]{2,1,0:T(8,128)}, u32[]{:S(2)}) copy-start(f32[2,32,1024]{2,1,0:T(8,128)} %param.21) | copy-start | bytes 786436
  7.2 32.8 %copy-start.42 = (s32[2]{0:T(128)S(1)}, s32[2]{0:T(128)}, u32[]{:S(2)}) copy-start(s32[2]{0:T(128)} %param.25) | copy-start | bytes 28
  7.2 240.1 %all-reduce.11.cloned.1.call-start = ((), (), s32[]{:S(2)}) async-start(), calls=%async_computation | async-start | bytes 262144 | tf_op jit(solution)/shard_map/psum | solution.py:166
  8.0 21.3 %collective-permute-start.18 = (f32[1,1,128]{2,1,0:T(1,128)S(1)}, f32[1,1,128]{2,1,0:T(1,128)S(1)}, u32[]{:S(2)}, u32[]{:S(2)}) collective-permute-start(f32[1,1,128]{2,1,0:T(1,128)S(1)} %get-tuple-element.591), channel_id=1, source_target_pairs={{0,2},{2,4},{4,6},{1,3},{3,5},{5,7},{8,10},{10,12},{12,14},{9,11},... | collective-permute-start | bytes 1544 | tf_op jit(solution)/shard_map/ppermute | solution.py:18
  13.0 16.3 %collective-permute-start.19 = (f32[1,1,128]{2,1,0:T(1,128)S(1)}, f32[1,1,128]{2,1,0:T(1,128)S(1)}, u32[]{:S(2)}, u32[]{:S(2)}) collective-permute-start(f32[1,1,128]{2,1,0:T(1,128)S(1)} %get-tuple-element.592), channel_id=1, source_target_pairs={{2,0},{4,2},{6,4},{3,1},{5,3},{7,5},{10,8},{12,10},{14,12},{11,9},... | collective-permute-start | bytes 1544 | tf_op jit(solution)/shard_map/ppermute | solution.py:21
  15.2 22.1 %collective-permute-start.4 = (f32[16,1024]{1,0:T(8,128)S(1)}, f32[16,1024]{1,0:T(8,128)S(1)}, u32[]{:S(2)}, u32[]{:S(2)}) collective-permute-start(f32[16,1024]{1,0:T(8,128)S(1)} %get-tuple-element.563), channel_id=1, source_target_pairs={{0,2},{2,4},{4,6},{1,3},{3,5},{5,7},{8,10},{10,12},{12,14},{9,11},... | collective-permute-start | bytes 196616 | tf_op jit(solution)/shard_map/ppermute | solution.py:18
  19.8 17.6 %collective-permute-start.5 = (f32[16,1024]{1,0:T(8,128)S(1)}, f32[16,1024]{1,0:T(8,128)S(1)}, u32[]{:S(2)}, u32[]{:S(2)}) collective-permute-start(f32[16,1024]{1,0:T(8,128)S(1)} %get-tuple-element.564), channel_id=1, source_target_pairs={{2,0},{4,2},{6,4},{3,1},{5,3},{7,5},{10,8},{12,10},{14,12},{11,9},... | collective-permute-start | bytes 196616 | tf_op jit(solution)/shard_map/ppermute | solution.py:21
  30.1 162.0 %collective-permute-start.21 = (f32[1,34,1]{2,1,0:T(8,128)S(1)}, f32[1,34,1]{2,1,0:T(8,128)S(1)}, u32[]{:S(2)}, u32[]{:S(2)}) collective-permute-start(f32[1,34,1]{2,1,0:T(8,128)S(1)} %get-tuple-element.585), channel_id=1, source_target_pairs={{1,0},{8,1},{9,8},{16,9},{17,16},{24,17},{25,24},{3,2},{10,3},{11,... | collective-permute-start | bytes 416 | tf_op jit(solution)/shard_map/ppermute | solution.py:21
  31.4 160.7 %collective-permute-start.20 = (f32[1,34,1]{2,1,0:T(8,128)S(1)}, f32[1,34,1]{2,1,0:T(8,128)S(1)}, u32[]{:S(2)}, u32[]{:S(2)}) collective-permute-start(f32[1,34,1]{2,1,0:T(8,128)S(1)} %get-tuple-element.586), channel_id=1, source_target_pairs={{0,1},{1,8},{8,9},{9,16},{16,17},{17,24},{24,25},{2,3},{3,10},{10,... | collective-permute-start | bytes 416 | tf_op jit(solution)/shard_map/ppermute | solution.py:18
  40.0 10.6 %collective-permute-start = (f32[2,2,16,1024]{3,2,1,0:T(8,128)S(1)}, f32[2,2,16,1024]{3,2,1,0:T(8,128)S(1)}, u32[]{:S(2)}, u32[]{:S(2)}) collective-permute-start(f32[2,2,16,1024]{3,2,1,0:T(8,128)S(1)} %get-tuple-element.760), channel_id=1, source_target_pairs={{2,0},{4,2},{6,4},{3,1},{5,3},{7,5},{10,8},{12,10},{14,12},{11,9},... | collective-permute-start | bytes 786440 | tf_op jit(solution)/shard_map/while/body/eval_jaxpr/ppermute | solution.py:21
  41.3 10.5 %collective-permute-start.1 = (f32[2,2,16,1024]{3,2,1,0:T(8,128)S(1)}, f32[2,2,16,1024]{3,2,1,0:T(8,128)S(1)}, u32[]{:S(2)}, u32[]{:S(2)}) collective-permute-start(f32[2,2,16,1024]{3,2,1,0:T(8,128)S(1)} %get-tuple-element.761), channel_id=1, source_target_pairs={{0,2},{2,4},{4,6},{1,3},{3,5},{5,7},{8,10},{10,12},{12,14},{9,11},... | collective-permute-start | bytes 786440 | tf_op jit(solution)/shard_map/while/body/eval_jaxpr/ppermute | solution.py:18
  56.7 9.6 %collective-permute-start = (f32[2,2,16,1024]{3,2,1,0:T(8,128)S(1)}, f32[2,2,16,1024]{3,2,1,0:T(8,128)S(1)}, u32[]{:S(2)}, u32[]{:S(2)}) collective-permute-start(f32[2,2,16,1024]{3,2,1,0:T(8,128)S(1)} %get-tuple-element.760), channel_id=1, source_target_pairs={{2,0},{4,2},{6,4},{3,1},{5,3},{7,5},{10,8},{12,10},{14,12},{11,9},... | collective-permute-start | bytes 786440 | tf_op jit(solution)/shard_map/while/body/eval_jaxpr/ppermute | solution.py:21
  58.0 9.5 %collective-permute-start.1 = (f32[2,2,16,1024]{3,2,1,0:T(8,128)S(1)}, f32[2,2,16,1024]{3,2,1,0:T(8,128)S(1)}, u32[]{:S(2)}, u32[]{:S(2)}) collective-permute-start(f32[2,2,16,1024]{3,2,1,0:T(8,128)S(1)} %get-tuple-element.761), channel_id=1, source_target_pairs={{0,2},{2,4},{4,6},{1,3},{3,5},{5,7},{8,10},{10,12},{12,14},{9,11},... | collective-permute-start | bytes 786440 | tf_op jit(solution)/shard_map/while/body/eval_jaxpr/ppermute | solution.py:18
  72.4 8.8 %collective-permute-start = (f32[2,2,16,1024]{3,2,1,0:T(8,128)S(1)}, f32[2,2,16,1024]{3,2,1,0:T(8,128)S(1)}, u32[]{:S(2)}, u32[]{:S(2)}) collective-permute-start(f32[2,2,16,1024]{3,2,1,0:T(8,128)S(1)} %get-tuple-element.760), channel_id=1, source_target_pairs={{2,0},{4,2},{6,4},{3,1},{5,3},{7,5},{10,8},{12,10},{14,12},{11,9},... | collective-permute-start | bytes 786440 | tf_op jit(solution)/shard_map/while/body/eval_jaxpr/ppermute | solution.py:21
  73.7 8.9 %collective-permute-start.1 = (f32[2,2,16,1024]{3,2,1,0:T(8,128)S(1)}, f32[2,2,16,1024]{3,2,1,0:T(8,128)S(1)}, u32[]{:S(2)}, u32[]{:S(2)}) collective-permute-start(f32[2,2,16,1024]{3,2,1,0:T(8,128)S(1)} %get-tuple-element.761), channel_id=1, source_target_pairs={{0,2},{2,4},{4,6},{1,3},{3,5},{5,7},{8,10},{10,12},{12,14},{9,11},... | collective-permute-start | bytes 786440 | tf_op jit(solution)/shard_map/while/body/eval_jaxpr/ppermute | solution.py:18
  87.5 8.7 %collective-permute-start = (f32[2,2,16,1024]{3,2,1,0:T(8,128)S(1)}, f32[2,2,16,1024]{3,2,1,0:T(8,128)S(1)}, u32[]{:S(2)}, u32[]{:S(2)}) collective-permute-start(f32[2,2,16,1024]{3,2,1,0:T(8,128)S(1)} %get-tuple-element.760), channel_id=1, source_target_pairs={{2,0},{4,2},{6,4},{3,1},{5,3},{7,5},{10,8},{12,10},{14,12},{11,9},... | collective-permute-start | bytes 786440 | tf_op jit(solution)/shard_map/while/body/eval_jaxpr/ppermute | solution.py:21
  88.8 8.9 %collective-permute-start.1 = (f32[2,2,16,1024]{3,2,1,0:T(8,128)S(1)}, f32[2,2,16,1024]{3,2,1,0:T(8,128)S(1)}, u32[]{:S(2)}, u32[]{:S(2)}) collective-permute-start(f32[2,2,16,1024]{3,2,1,0:T(8,128)S(1)} %get-tuple-element.761), channel_id=1, source_target_pairs={{0,2},{2,4},{4,6},{1,3},{3,5},{5,7},{8,10},{10,12},{12,14},{9,11},... | collective-permute-start | bytes 786440 | tf_op jit(solution)/shard_map/while/body/eval_jaxpr/ppermute | solution.py:18
  110.4 10.7 %collective-permute-start.2 = (f32[2,2,16,1024]{3,2,1,0:T(8,128)S(1)}, f32[2,2,16,1024]{3,2,1,0:T(8,128)S(1)}, u32[]{:S(2)}, u32[]{:S(2)}) collective-permute-start(f32[2,2,16,1024]{3,2,1,0:T(8,128)S(1)} %get-tuple-element.783), channel_id=1, source_target_pairs={{2,0},{4,2},{6,4},{3,1},{5,3},{7,5},{10,8},{12,10},{14,12},{11,9},... | collective-permute-start | bytes 786440 | tf_op jit(solution)/shard_map/while/body/eval_jaxpr/ppermute | solution.py:21
  111.7 9.5 %collective-permute-start.3 = (f32[2,2,16,1024]{3,2,1,0:T(8,128)S(1)}, f32[2,2,16,1024]{3,2,1,0:T(8,128)S(1)}, u32[]{:S(2)}, u32[]{:S(2)}) collective-permute-start(f32[2,2,16,1024]{3,2,1,0:T(8,128)S(1)} %get-tuple-element.784), channel_id=1, source_target_pairs={{0,2},{2,4},{4,6},{1,3},{3,5},{5,7},{8,10},{10,12},{12,14},{9,11},... | collective-permute-start | bytes 786440 | tf_op jit(solution)/shard_map/while/body/eval_jaxpr/ppermute | solution.py:18
  126.0 10.3 %collective-permute-start.2 = (f32[2,2,16,1024]{3,2,1,0:T(8,128)S(1)}, f32[2,2,16,1024]{3,2,1,0:T(8,128)S(1)}, u32[]{:S(2)}, u32[]{:S(2)}) collective-permute-start(f32[2,2,16,1024]{3,2,1,0:T(8,128)S(1)} %get-tuple-element.783), channel_id=1, source_target_pairs={{2,0},{4,2},{6,4},{3,1},{5,3},{7,5},{10,8},{12,10},{14,12},{11,9},... | collective-permute-start | bytes 786440 | tf_op jit(solution)/shard_map/while/body/eval_jaxpr/ppermute | solution.py:21
  127.3 9.0 %collective-permute-start.3 = (f32[2,2,16,1024]{3,2,1,0:T(8,128)S(1)}, f32[2,2,16,1024]{3,2,1,0:T(8,128)S(1)}, u32[]{:S(2)}, u32[]{:S(2)}) collective-permute-start(f32[2,2,16,1024]{3,2,1,0:T(8,128)S(1)} %get-tuple-element.784), channel_id=1, source_target_pairs={{0,2},{2,4},{4,6},{1,3},{3,5},{5,7},{8,10},{10,12},{12,14},{9,11},... | collective-permute-start | bytes 786440 | tf_op jit(solution)/shard_map/while/body/eval_jaxpr/ppermute | solution.py:18
  141.2 10.3 %collective-permute-start.2 = (f32[2,2,16,1024]{3,2,1,0:T(8,128)S(1)}, f32[2,2,16,1024]{3,2,1,0:T(8,128)S(1)}, u32[]{:S(2)}, u32[]{:S(2)}) collective-permute-start(f32[2,2,16,1024]{3,2,1,0:T(8,128)S(1)} %get-tuple-element.783), channel_id=1, source_target_pairs={{2,0},{4,2},{6,4},{3,1},{5,3},{7,5},{10,8},{12,10},{14,12},{11,9},... | collective-permute-start | bytes 786440 | tf_op jit(solution)/shard_map/while/body/eval_jaxpr/ppermute | solution.py:21
  142.5 9.0 %collective-permute-start.3 = (f32[2,2,16,1024]{3,2,1,0:T(8,128)S(1)}, f32[2,2,16,1024]{3,2,1,0:T(8,128)S(1)}, u32[]{:S(2)}, u32[]{:S(2)}) collective-permute-start(f32[2,2,16,1024]{3,2,1,0:T(8,128)S(1)} %get-tuple-element.784), channel_id=1, source_target_pairs={{0,2},{2,4},{4,6},{1,3},{3,5},{5,7},{8,10},{10,12},{12,14},{9,11},... | collective-permute-start | bytes 786440 | tf_op jit(solution)/shard_map/while/body/eval_jaxpr/ppermute | solution.py:18
  156.4 10.3 %collective-permute-start.2 = (f32[2,2,16,1024]{3,2,1,0:T(8,128)S(1)}, f32[2,2,16,1024]{3,2,1,0:T(8,128)S(1)}, u32[]{:S(2)}, u32[]{:S(2)}) collective-permute-start(f32[2,2,16,1024]{3,2,1,0:T(8,128)S(1)} %get-tuple-element.783), channel_id=1, source_target_pairs={{2,0},{4,2},{6,4},{3,1},{5,3},{7,5},{10,8},{12,10},{14,12},{11,9},... | collective-permute-start | bytes 786440 | tf_op jit(solution)/shard_map/while/body/eval_jaxpr/ppermute | solution.py:21
  157.7 9.0 %collective-permute-start.3 = (f32[2,2,16,1024]{3,2,1,0:T(8,128)S(1)}, f32[2,2,16,1024]{3,2,1,0:T(8,128)S(1)}, u32[]{:S(2)}, u32[]{:S(2)}) collective-permute-start(f32[2,2,16,1024]{3,2,1,0:T(8,128)S(1)} %get-tuple-element.784), channel_id=1, source_target_pairs={{0,2},{2,4},{4,6},{1,3},{3,5},{5,7},{8,10},{10,12},{12,14},{9,11},... | collective-permute-start | bytes 786440 | tf_op jit(solution)/shard_map/while/body/eval_jaxpr/ppermute | solution.py:18
  185.0 7.1 %copy-start.34 = (f32[32,128]{1,0:T(8,128)S(1)}, f32[32,128]{1,0:T(8,128)}, u32[]{:S(2)}) copy-start(f32[32,128]{1,0:T(8,128)} %param.33) | copy-start | bytes 49156
  192.0 81.2 %copy-start.39 = (f32[1,32,128]{2,1,0:T(8,128)S(1)}, f32[1,32,128]{2,1,0:T(8,128)}, u32[]{:S(2)}) copy-start(f32[1,32,128]{2,1,0:T(8,128)} %get-tuple-element.589) | copy-start | bytes 49156
  192.0 81.2 %copy-start.40 = (f32[1,32,128]{2,1,0:T(8,128)S(1)}, f32[1,32,128]{2,1,0:T(8,128)}, u32[]{:S(2)}) copy-start(f32[1,32,128]{2,1,0:T(8,128)} %get-tuple-element.590) | copy-start | bytes 49156
  248.0 5.4 %collective-permute-start.6 = (f32[2,1,128]{2,1,0:T(1,128)S(1)}, f32[2,1,128]{2,1,0:T(1,128)S(1)}, u32[]{:S(2)}, u32[]{:S(2)}) collective-permute-start(f32[2,1,128]{2,1,0:T(1,128)S(1)} %get-tuple-element.583), channel_id=1, source_target_pairs={{0,2},{2,4},{4,6},{1,3},{3,5},{5,7},{8,10},{10,12},{12,14},{9,11},... | collective-permute-start | bytes 3080 | tf_op jit(solution)/shard_map/ppermute | solution.py:18
  251.4 5.5 %collective-permute-start.7 = (f32[2,1,128]{2,1,0:T(1,128)S(1)}, f32[2,1,128]{2,1,0:T(1,128)S(1)}, u32[]{:S(2)}, u32[]{:S(2)}) collective-permute-start(f32[2,1,128]{2,1,0:T(1,128)S(1)} %get-tuple-element.584), channel_id=1, source_target_pairs={{2,0},{4,2},{6,4},{3,1},{5,3},{7,5},{10,8},{12,10},{14,12},{11,9},... | collective-permute-start | bytes 3080 | tf_op jit(solution)/shard_map/ppermute | solution.py:21
  257.0 5.9 %collective-permute-start.9 = (f32[2,34,1]{2,1,0:T(8,128)S(1)}, f32[2,34,1]{2,1,0:T(8,128)S(1)}, u32[]{:S(2)}, u32[]{:S(2)}) collective-permute-start(f32[2,34,1]{2,1,0:T(8,128)S(1)} %get-tuple-element.577), channel_id=1, source_target_pairs={{1,0},{8,1},{9,8},{16,9},{17,16},{24,17},{25,24},{3,2},{10,3},{11,... | collective-permute-start | bytes 824 | tf_op jit(solution)/shard_map/ppermute | solution.py:21
  258.3 6.2 %collective-permute-start.8 = (f32[2,34,1]{2,1,0:T(8,128)S(1)}, f32[2,34,1]{2,1,0:T(8,128)S(1)}, u32[]{:S(2)}, u32[]{:S(2)}) collective-permute-start(f32[2,34,1]{2,1,0:T(8,128)S(1)} %get-tuple-element.578), channel_id=1, source_target_pairs={{0,1},{1,8},{8,9},{9,16},{16,17},{17,24},{24,25},{2,3},{3,10},{10,... | collective-permute-start | bytes 824 | tf_op jit(solution)/shard_map/ppermute | solution.py:18
  266.7 13.5 %collective-permute-start.11 = (f32[32,1,128]{2,0,1:T(8,128)}, f32[32,1,128]{2,0,1:T(8,128)S(1)}, u32[]{:S(2)}, u32[]{:S(2)}) collective-permute-start(f32[32,1,128]{2,0,1:T(8,128)} %bitcast.93), channel_id=1, source_target_pairs={{2,0},{4,2},{6,4},{3,1},{5,3},{7,5},{10,8},{12,10},{14,12},{11,9},... | collective-permute-start | bytes 49160 | tf_op jit(solution)/shard_map/ppermute | solution.py:21
  268.0 8.6 %collective-permute-start.10 = (f32[32,1,128]{2,0,1:T(8,128)}, f32[32,1,128]{2,0,1:T(8,128)}, u32[]{:S(2)}, u32[]{:S(2)}) collective-permute-start(f32[32,1,128]{2,0,1:T(8,128)} %bitcast.92), channel_id=1, source_target_pairs={{0,2},{2,4},{4,6},{1,3},{3,5},{5,7},{8,10},{10,12},{12,14},{9,11},... | collective-permute-start | bytes 49160 | tf_op jit(solution)/shard_map/ppermute | solution.py:18
  276.5 7.5 %copy-start.8 = (f32[32,32,128]{1,0,2:T(8,128)}, f32[32,32,128]{1,0,2:T(8,128)S(1)}, u32[]{:S(2)}) copy-start(f32[32,32,128]{1,0,2:T(8,128)S(1)} %copy.126) | copy-start | bytes 1572868
  283.0 9.8 %copy-start.11 = (f32[32,1,128]{1,0,2:T(8,128)S(1)}, f32[32,1,128]{1,0,2:T(8,128)}, u32[]{:S(2)}) copy-start(f32[32,1,128]{1,0,2:T(8,128)} %copy.125) | copy-start | bytes 49156
  283.0 9.8 %copy-start.12 = (f32[32,1,128]{1,0,2:T(8,128)S(1)}, f32[32,1,128]{1,0,2:T(8,128)}, u32[]{:S(2)}) copy-start(f32[32,1,128]{1,0,2:T(8,128)} %copy.127) | copy-start | bytes 49156
  284.0 8.7 %collective-permute-start.13 = (f32[32,34,1]{1,0,2:T(8,128)S(1)}, f32[32,34,1]{1,0,2:T(8,128)S(1)}, u32[]{:S(2)}, u32[]{:S(2)}) collective-permute-start(f32[32,34,1]{1,0,2:T(8,128)S(1)} %get-tuple-element.531), channel_id=1, source_target_pairs={{1,0},{8,1},{9,8},{16,9},{17,16},{24,17},{25,24},{3,2},{10,3},{11,... | collective-permute-start | bytes 13064 | tf_op jit(solution)/shard_map/ppermute | solution.py:21
  285.5 7.3 %collective-permute-start.12 = (f32[32,34,1]{1,0,2:T(8,128)S(1)}, f32[32,34,1]{1,0,2:T(8,128)S(1)}, u32[]{:S(2)}, u32[]{:S(2)}) collective-permute-start(f32[32,34,1]{1,0,2:T(8,128)S(1)} %get-tuple-element.532), channel_id=1, source_target_pairs={{0,1},{1,8},{8,9},{9,16},{16,17},{17,24},{24,25},{2,3},{3,10},{10,... | collective-permute-start | bytes 13064 | tf_op jit(solution)/shard_map/ppermute | solution.py:18
  324.3 7.2 %copy-start.32 = (f32[32,32,128]{2,1,0:T(8,128)S(1)}, f32[32,32,128]{2,1,0:T(8,128)}, u32[]{:S(2)}) copy-start(f32[32,32,128]{2,1,0:T(8,128)} %copy.133) | copy-start | bytes 1572868
  324.3 7.5 %copy-start.27 = (f32[32,32,128]{2,1,0:T(8,128)S(1)}, f32[32,32,128]{2,1,0:T(8,128)}, u32[]{:S(2)}) copy-start(f32[32,32,128]{2,1,0:T(8,128)} %get-tuple-element.559) | copy-start | bytes 1572868
  324.3 7.9 %copy-start.29 = (f32[32,32,128]{2,1,0:T(8,128)S(1)}, f32[32,32,128]{2,1,0:T(8,128)}, u32[]{:S(2)}) copy-start(f32[32,32,128]{2,1,0:T(8,128)} %copy.135) | copy-start | bytes 1572868
  342.9 22.8 %collective-permute-start.15 = (f32[32,1,128]{2,0,1:T(8,128)}, f32[32,1,128]{2,0,1:T(8,128)S(1)}, u32[]{:S(2)}, u32[]{:S(2)}) collective-permute-start(f32[32,1,128]{2,0,1:T(8,128)} %bitcast.95), channel_id=1, source_target_pairs={{2,0},{4,2},{6,4},{3,1},{5,3},{7,5},{10,8},{12,10},{14,12},{11,9},... | collective-permute-start | bytes 49160 | tf_op jit(solution)/shard_map/ppermute | solution.py:21
  344.2 17.9 %collective-permute-start.14 = (f32[32,1,128]{2,0,1:T(8,128)}, f32[32,1,128]{2,0,1:T(8,128)}, u32[]{:S(2)}, u32[]{:S(2)}) collective-permute-start(f32[32,1,128]{2,0,1:T(8,128)} %bitcast.94), channel_id=1, source_target_pairs={{0,2},{2,4},{4,6},{1,3},{3,5},{5,7},{8,10},{10,12},{12,14},{9,11},... | collective-permute-start | bytes 49160 | tf_op jit(solution)/shard_map/ppermute | solution.py:18
  355.6 14.4 %copy-start.6 = (f32[32,32,128]{1,0,2:T(8,128)}, f32[32,32,128]{1,0,2:T(8,128)S(1)}, u32[]{:S(2)}) copy-start(f32[32,32,128]{1,0,2:T(8,128)S(1)} %copy.139) | copy-start | bytes 1572868
  355.7 24.5 %collective-permute-start.23 = (f32[32,1,128]{2,0,1:T(8,128)}, f32[32,1,128]{2,0,1:T(8,128)}, u32[]{:S(2)}, u32[]{:S(2)}) collective-permute-start(f32[32,1,128]{2,0,1:T(8,128)} %bitcast.436), channel_id=1, source_target_pairs={{2,0},{4,2},{6,4},{3,1},{5,3},{7,5},{10,8},{12,10},{14,12},{11,9},... | collective-permute-start | bytes 49160 | tf_op jit(solution)/shard_map/ppermute | solution.py:21
  357.0 19.7 %collective-permute-start.22 = (f32[32,1,128]{2,0,1:T(8,128)}, f32[32,1,128]{2,0,1:T(8,128)}, u32[]{:S(2)}, u32[]{:S(2)}) collective-permute-start(f32[32,1,128]{2,0,1:T(8,128)} %bitcast.437), channel_id=1, source_target_pairs={{0,2},{2,4},{4,6},{1,3},{3,5},{5,7},{8,10},{10,12},{12,14},{9,11},... | collective-permute-start | bytes 49160 | tf_op jit(solution)/shard_map/ppermute | solution.py:18
  370.1 13.7 %copy-start.7 = (f32[32,32,128]{1,0,2:T(8,128)S(1)}, f32[32,32,128]{1,0,2:T(8,128)}, u32[]{:S(2)}) copy-start(f32[32,32,128]{1,0,2:T(8,128)} %copy.152) | copy-start | bytes 1572868
  370.1 40.7 %collective-permute-start.17 = (f32[32,34,1]{1,0,2:T(8,128)}, f32[32,34,1]{1,0,2:T(8,128)}, u32[]{:S(2)}, u32[]{:S(2)}) collective-permute-start(f32[32,34,1]{1,0,2:T(8,128)} %get-tuple-element.527), channel_id=1, source_target_pairs={{1,0},{8,1},{9,8},{16,9},{17,16},{24,17},{25,24},{3,2},{10,3},{11,... | collective-permute-start | bytes 13064 | tf_op jit(solution)/shard_map/ppermute | solution.py:21
  371.5 39.3 %collective-permute-start.16 = (f32[32,34,1]{1,0,2:T(8,128)}, f32[32,34,1]{1,0,2:T(8,128)}, u32[]{:S(2)}, u32[]{:S(2)}) collective-permute-start(f32[32,34,1]{1,0,2:T(8,128)} %get-tuple-element.528), channel_id=1, source_target_pairs={{0,1},{1,8},{8,9},{9,16},{16,17},{17,24},{24,25},{2,3},{3,10},{10,... | collective-permute-start | bytes 13064 | tf_op jit(solution)/shard_map/ppermute | solution.py:18
  383.8 7.4 %copy-start.16 = (f32[4,8,32,128]{3,2,1,0:T(8,128)S(1)}, f32[4,8,32,128]{3,2,1,0:T(8,128)}, u32[]{:S(2)}) copy-start(f32[4,8,32,128]{3,2,1,0:T(8,128)} %copy-done.15) | copy-start | bytes 1572868
  383.8 11.2 %copy-start.9 = (f32[32,1,128]{1,0,2:T(8,128)S(1)}, f32[32,1,128]{1,0,2:T(8,128)}, u32[]{:S(2)}) copy-start(f32[32,1,128]{1,0,2:T(8,128)} %copy.151) | copy-start | bytes 49156
  383.8 11.2 %copy-start.10 = (f32[32,1,128]{1,0,2:T(8,128)S(1)}, f32[32,1,128]{1,0,2:T(8,128)}, u32[]{:S(2)}) copy-start(f32[32,1,128]{1,0,2:T(8,128)} %copy.153) | copy-start | bytes 49156
  384.8 10.1 %collective-permute-start.25 = (f32[32,34,1]{1,0,2:T(8,128)S(1)}, f32[32,34,1]{1,0,2:T(8,128)S(1)}, u32[]{:S(2)}, u32[]{:S(2)}) collective-permute-start(f32[32,34,1]{1,0,2:T(8,128)S(1)} %get-tuple-element.523), channel_id=1, source_target_pairs={{1,0},{8,1},{9,8},{16,9},{17,16},{24,17},{25,24},{3,2},{10,3},{11,... | collective-permute-start | bytes 13064 | tf_op jit(solution)/shard_map/ppermute | solution.py:21
  386.3 8.7 %collective-permute-start.24 = (f32[32,34,1]{1,0,2:T(8,128)S(1)}, f32[32,34,1]{1,0,2:T(8,128)S(1)}, u32[]{:S(2)}, u32[]{:S(2)}) collective-permute-start(f32[32,34,1]{1,0,2:T(8,128)S(1)} %get-tuple-element.524), channel_id=1, source_target_pairs={{0,1},{1,8},{8,9},{9,16},{16,17},{17,24},{24,25},{2,3},{3,10},{10,... | collective-permute-start | bytes 13064 | tf_op jit(solution)/shard_map/ppermute | solution.py:18
  442.5 12.6 %copy-start.20 = (f32[32,4096]{1,0:T(8,128)S(1)}, f32[32,4096]{1,0:T(8,128)}, u32[]{:S(2)}) copy-start(f32[32,4096]{1,0:T(8,128)} %copy-done.19) | copy-start | bytes 1572868
  464.9 7.1 %copy-start.14 = (f32[32,32,128]{1,0,2:T(8,128)S(1)}, f32[32,32,128]{1,0,2:T(8,128)}, u32[]{:S(2)}) copy-start(f32[32,32,128]{1,0,2:T(8,128)} %get-tuple-element.544) | copy-start | bytes 1572868
  464.9 10.7 %copy-start.22 = (f32[32,32,128]{2,1,0:T(8,128)S(1)}, f32[32,32,128]{2,1,0:T(8,128)}, u32[]{:S(2)}) copy-start(f32[32,32,128]{2,1,0:T(8,128)} %get-tuple-element.556) | copy-start | bytes 1572868
  468.5 10.1 %copy-start.18 = (f32[32,4096]{1,0:T(8,128)S(1)}, f32[32,4096]{1,0:T(8,128)}, u32[]{:S(2)}) copy-start(f32[32,4096]{1,0:T(8,128)} %copy-done.17) | copy-start | bytes 1572868
  479.8 47.3 %copy-start.1 = (f32[32,18]{0,1:T(8,128)S(1)}, f32[32,18]{0,1:T(8,128)}, u32[]{:S(2)}) copy-start(f32[32,18]{0,1:T(8,128)} %param.30) | copy-start | bytes 6916
  480.2 7.8 %copy-start.38 = (f32[32,288]{1,0:T(8,128)S(1)}, f32[32,288]{1,0:T(8,128)}, u32[]{:S(2)}) copy-start(f32[32,288]{1,0:T(8,128)} %fusion.230) | copy-start | bytes 110596
  480.2 7.7 %copy-start.41 = (f32[32,18]{0,1:T(8,128)S(1)}, f32[32,18]{0,1:T(8,128)}, u32[]{:S(2)}) copy-start(f32[32,18]{0,1:T(8,128)} %fusion.229) | copy-start | bytes 6916
  (21 other events, 104.4 us)
Sparse Core Ops, SparseCore 0:
  192.2 55.0 all-reduce.10
where the time goes:
time: 544 us; the launch traced here: 534 us
  local copies, waits for them, and re-layouts  169 us (31%)
  starting transfers between devices  117 us (22%)
  other arithmetic  78.2 us (14%)
  waiting for transfers between devices  76.8 us (14%)
  blocking collectives  39.2 us (7%)
  matrix products  37.4 us (7%)
  between operations  15.3 us (3%)
    ppermute x19, starting transfers between devices, extended_2(): lax.ppermute(lax.slice_in_dim(block, block.shape[dim] - width, None, axis...  91.8 us
    slice x25, local copies, waits for them, and re-layouts, patches(): extended[:, down:down + height, across:across + breadth]  83.9 us
    psum x1, waiting for transfers between devices, on_device(): gathered = lax.psum(imaging, ('shot', 'net'))  55.1 us
    psum x1, blocking collectives, on_device(): totals = lax.psum((grad_in, grad_mid, grad_out), ('shot', 'band', 'net'))  39.2 us
    concatenate x23, other arithmetic, extended_2(): block = jnp.concatenate([low, block, high], axis=dim)  27.2 us
    ppermute x19, starting transfers between devices, extended_2(): lax.ppermute(lax.slice_in_dim(block, 0, width, axis=dim), axis, backward)  24.9 us
    unnamed x126, local copies, waits for them, and re-layouts  22.8 us
    add x24, other arithmetic, block(): 2.0 * current[:, 4:-4] - earlier[:, 4:-4] + speed_part * laplace(current)  21.6 us
  transfers between devices with their start and end apart: 39, of which 11 were waited for; matrix products, arithmetic and copies ran while one was open for 28% of the time, Pallas kernels for 0%

commit v1 on v0

--- a/solution.py
+++ b/solution.py
@@ -1,6 +1,11 @@
+import functools
+
 import jax
 import jax.numpy as jnp
+import numpy as np
 from jax import lax
+from jax.experimental import pallas as pl
+from jax.experimental.pallas import tpu as pltpu
 from jax.sharding import PartitionSpec as P
 
 coefficients = (-205.0 / 72.0, 8.0 / 5.0, -1.0 / 5.0, 8.0 / 315.0, -1.0 / 560.0)
@@ -54,15 +59,6 @@
     return ((columns[None, :, None] == placed[:, None, :]) & active[:, None, :]).astype(jnp.float32)
 
 
-def patches(extended, height, breadth):
-    parts = [
-        extended[:, down : down + height, across : across + breadth]
-        for down in range(3)
-        for across in range(3)
-    ]
-    return jnp.concatenate(parts, 0).reshape(-1, height * breadth)
-
-
 def flipped(weights):
     outputs = weights.shape[0]
     channels = weights.shape[1] // 9
@@ -73,17 +69,458 @@
     )
 
 
-def sigmoid_slope(values):
-    squashed = jax.nn.sigmoid(values)
-    return squashed * (1.0 + values * (1.0 - squashed))
-
-
-def matmul(left, right):
-    return jnp.dot(left, right, precision=highest)
-
-
-def outer_sum(left, right):
-    return lax.dot_general(left, right, (((1,), (1,)), ((), ())), precision=highest)
+MESH = pl.DeviceIdType.MESH
+group_axes = ("shot", "net")
+chunk = 512
+
+
+def vmem(count):
+    return [pl.BlockSpec(memory_space=pltpu.VMEM)] * count
+
+
+def remote(source, target, send, receive, device):
+    return pltpu.make_async_remote_copy(
+        src_ref=source,
+        dst_ref=target,
+        send_sem=send,
+        recv_sem=receive,
+        device_id=device,
+        device_id_type=MESH,
+    )
+
+
+def gather_kernel(
+    groups, nets, bands, image, velocity, cotangent,
+    out_image, out_cot, out_low, out_high,
+    padded, slots, total, halo, speed_halo,
+    send, receive, side_send, side_receive, row_send, row_receive,
+):
+    rows, breadth = image.shape
+    piece = cotangent.shape[1]
+    shot = lax.axis_index("shot")
+    net = lax.axis_index("net")
+    band = lax.axis_index("band")
+    me = shot * nets + net
+
+    def member(index):
+        return {"shot": index // nets, "net": lax.rem(index, nets)}
+
+    total[1] = jnp.zeros((rows, 3 * piece), jnp.float32)
+    halo[...] = jnp.zeros(halo.shape, jnp.float32)
+    speed_halo[...] = jnp.zeros(speed_halo.shape, jnp.float32)
+    barrier = pltpu.get_barrier_semaphore()
+    for step in range(1, groups):
+        pl.semaphore_signal(
+            barrier, inc=1, device_id=member(lax.rem(me + step, groups)), device_id_type=MESH
+        )
+
+    @pl.when(band > 0)
+    def _():
+        pl.semaphore_signal(barrier, inc=1, device_id={"band": band - 1}, device_id_type=MESH)
+
+    @pl.when(band < bands - 1)
+    def _():
+        pl.semaphore_signal(barrier, inc=1, device_id={"band": band + 1}, device_id_type=MESH)
+
+    padded[:, :piece] = jnp.zeros((rows, piece), jnp.float32)
+    padded[:, piece + breadth :] = jnp.zeros((rows, piece), jnp.float32)
+    padded[:, piece : piece + breadth] = image[...]
+    pl.semaphore_wait(
+        barrier, groups - 1 + lax.min(band, 1) + lax.min(bands - 1 - band, 1)
+    )
+
+    def scatter(step):
+        target = lax.rem(me + step, groups)
+        start = pl.multiple_of(target * piece, 128)
+        return remote(
+            padded.at[:, pl.ds(start, 3 * piece)],
+            slots.at[step],
+            send.at[step],
+            receive.at[step],
+            member(target),
+        )
+
+    for step in range(1, groups):
+        scatter(step).start()
+
+    def to_right():
+        return remote(
+            cotangent, total.at[1, :, pl.ds(0, piece)], side_send.at[0], side_receive.at[0],
+            member(me + 1),
+        )
+
+    def to_left():
+        return remote(
+            cotangent, total.at[1, :, pl.ds(2 * piece, piece)], side_send.at[1],
+            side_receive.at[1], member(me - 1),
+        )
+
+    def speed_up():
+        return remote(
+            velocity.at[pl.ds(0, 8)], speed_halo.at[1], row_send.at[0], row_receive.at[0],
+            {"band": band - 1},
+        )
+
+    def speed_down():
+        return remote(
+            velocity.at[pl.ds(rows - 8, 8)], speed_halo.at[0], row_send.at[1], row_receive.at[1],
+            {"band": band + 1},
+        )
+
+    def field_up():
+        return remote(
+            total.at[:, pl.ds(0, 8)], halo.at[1], row_send.at[2], row_receive.at[2],
+            {"band": band - 1},
+        )
+
+    def field_down():
+        return remote(
+            total.at[:, pl.ds(rows - 8, 8)], halo.at[0], row_send.at[3], row_receive.at[3],
+            {"band": band + 1},
+        )
+
+    pl.when(me < groups - 1)(lambda: to_right().start())
+    pl.when(me > 0)(lambda: to_left().start())
+    pl.when(band > 0)(lambda: speed_up().start())
+    pl.when(band < bands - 1)(lambda: speed_down().start())
+
+    own = pl.multiple_of(me * piece, 128)
+    slots[0] = padded[:, pl.ds(own, 3 * piece)]
+    for step in range(1, groups):
+        scatter(step).wait_recv()
+    summed = slots[0]
+    for step in range(1, groups):
+        summed = summed + slots[step]
+    total[0] = summed
+    pl.when(me > 0)(lambda: to_right().wait_recv())
+    pl.when(me < groups - 1)(lambda: to_left().wait_recv())
+    total[1, :, piece : 2 * piece] = cotangent[...]
+    pl.when(band > 0)(lambda: field_up().start())
+    pl.when(band < bands - 1)(lambda: field_down().start())
+    for step in range(1, groups):
+        scatter(step).wait_send()
+    pl.when(me < groups - 1)(lambda: to_right().wait_send())
+    pl.when(me > 0)(lambda: to_left().wait_send())
+    pl.when(band > 0)(lambda: speed_up().wait_send())
+    pl.when(band < bands - 1)(lambda: speed_down().wait_send())
+    pl.when(band > 0)(lambda: speed_down().wait_recv())
+    pl.when(band < bands - 1)(lambda: speed_up().wait_recv())
+    pl.when(band > 0)(lambda: field_up().wait_send())
+    pl.when(band < bands - 1)(lambda: field_down().wait_send())
+    pl.when(band > 0)(lambda: field_down().wait_recv())
+    pl.when(band < bands - 1)(lambda: field_up().wait_recv())
+    for which, target in ((0, out_image), (1, out_cot)):
+        target[0:8] = halo[0, which]
+        target[8 : 8 + rows] = total[which]
+        target[8 + rows :] = halo[1, which]
+    out_low[...] = speed_halo[0]
+    out_high[...] = speed_halo[1]
+
+
+def gather_pieces(image, velocity, cotangent):
+    rows, breadth = image.shape
+    piece = cotangent.shape[1]
+    groups = lax.axis_size(group_axes)
+    nets = lax.axis_size("net")
+    bands = lax.axis_size("band")
+    f32 = jnp.float32
+    dma = pltpu.SemaphoreType.DMA
+    return pl.pallas_call(
+        functools.partial(gather_kernel, groups, nets, bands),
+        name="gather_pieces",
+        out_shape=[jax.ShapeDtypeStruct((rows + 16, 3 * piece), f32)] * 2
+        + [jax.ShapeDtypeStruct((8, breadth), f32)] * 2,
+        in_specs=vmem(3),
+        out_specs=vmem(4),
+        scratch_shapes=[
+            pltpu.VMEM((rows, breadth + 2 * piece), f32),
+            pltpu.VMEM((groups, rows, 3 * piece), f32),
+            pltpu.VMEM((2, rows, 3 * piece), f32),
+            pltpu.VMEM((2, 2, 8, 3 * piece), f32),
+            pltpu.VMEM((2, 8, breadth), f32),
+            dma((groups,)),
+            dma((groups,)),
+            dma((2,)),
+            dma((2,)),
+            dma((4,)),
+            dma((4,)),
+        ],
+        compiler_params=pltpu.CompilerParams(collective_id=1, has_side_effects=True),
+    )(image, velocity, cotangent)
+
+
+def total_kernel(sizes, grads, out, shot_slots, net_slots, band_slots, ready, send, receive):
+    part = grads.shape[0] // sizes["shot"]
+    barrier = pltpu.get_barrier_semaphore()
+    count = 0
+    for axis, size in sizes.items():
+        me = lax.axis_index(axis)
+        for step in range(1, size):
+            pl.semaphore_signal(
+                barrier, inc=1, device_id={axis: lax.rem(me + step, size)}, device_id_type=MESH
+            )
+            count += 1
+    pl.semaphore_wait(barrier, count)
+    base = 0
+
+    def stage(axis, source, target_of, base):
+        size = sizes[axis]
+        me = lax.axis_index(axis)
+
+        def copy(step, sender):
+            peer = lax.rem(me + step, size)
+            return remote(
+                source(peer), target_of(sender), send.at[base + step], receive.at[base + sender],
+                {axis: peer},
+            )
+
+        for step in range(1, size):
+            copy(step, me).start()
+        return copy, size, me
+
+    def finish(handle):
+        copy, size, me = handle
+        for step in range(1, size):
+            copy(step, lax.rem(me + step, size)).wait_recv()
+        for step in range(1, size):
+            copy(step, me).wait_send()
+
+    shot = lax.axis_index("shot")
+    handle = stage(
+        "shot",
+        lambda peer: grads.at[pl.ds(pl.multiple_of(peer * part, 8), part)],
+        lambda sender: shot_slots.at[sender],
+        0,
+    )
+    shot_slots[shot] = grads[pl.ds(pl.multiple_of(shot * part, 8), part)]
+    finish(handle)
+
+    def add(slots):
+        running = slots[0]
+        for index in range(1, slots.shape[0]):
+            running = running + slots[index]
+        return running
+
+    base = sizes["shot"]
+    ready[0] = add(shot_slots)
+    handle = stage("net", lambda peer: ready.at[0], lambda sender: net_slots.at[sender], base)
+    net_slots[lax.axis_index("net")] = ready[0]
+    finish(handle)
+    base += sizes["net"]
+    ready[1] = add(net_slots)
+    handle = stage("band", lambda peer: ready.at[1], lambda sender: band_slots.at[sender], base)
+    band_slots[lax.axis_index("band")] = ready[1]
+    finish(handle)
+    base += sizes["band"]
+    ready[2] = add(band_slots)
+    handle = stage(
+        "shot",
+        lambda peer: ready.at[2],
+        lambda sender: out.at[pl.ds(pl.multiple_of(sender * part, 8), part)],
+        base,
+    )
+    out[pl.ds(pl.multiple_of(shot * part, 8), part)] = ready[2]
+    finish(handle)
+
+
+def total_grads(grads):
+    sizes = {axis: lax.axis_size(axis) for axis in ("shot", "net", "band")}
+    part = (grads.shape[0] // sizes["shot"], grads.shape[1])
+    f32 = jnp.float32
+    count = 2 * sizes["shot"] + sizes["net"] + sizes["band"]
+    return pl.pallas_call(
+        functools.partial(total_kernel, sizes),
+        name="total_grads",
+        out_shape=jax.ShapeDtypeStruct(grads.shape, f32),
+        in_specs=vmem(1),
+        out_specs=vmem(1)[0],
+        scratch_shapes=[
+            pltpu.VMEM((sizes["shot"],) + part, f32),
+            pltpu.VMEM((sizes["net"],) + part, f32),
+            pltpu.VMEM((sizes["band"],) + part, f32),
+            pltpu.VMEM((3,) + part, f32),
+            pltpu.SemaphoreType.DMA((count,)),
+            pltpu.SemaphoreType.DMA((count,)),
+        ],
+        compiler_params=pltpu.CompilerParams(collective_id=2, has_side_effects=True),
+    )(grads)
+
+
+def halves(values):
+    high = values.astype(jnp.bfloat16)
+    return high, (values - high.astype(jnp.float32)).astype(jnp.bfloat16)
+
+
+def dot3(left, right_high, right_low, dims):
+    high, low = halves(left)
+    height = left.shape[0]
+    both = lax.dot_general(
+        jnp.concatenate([high, low], 0), right_high, (dims, ((), ())),
+        preferred_element_type=jnp.float32,
+    )
+    rest = lax.dot_general(
+        high, right_low, (dims, ((), ())), preferred_element_type=jnp.float32
+    )
+    return both[:height] + both[height:] + rest
+
+
+def network_kernel(
+    width, first, middle, middle_back, last, layers,
+    new_velocity, grads,
+    patch_zero, patch_high, patch_low, before_one, hidden, slope_two, last_taps,
+):
+    length = layers.shape[1]
+    channels = middle.shape[0]
+    shifts = [down * width + across for down in (-1, 0, 1) for across in (-1, 0, 1)]
+    pieces = length // chunk
+    flat = ((1,), (0,))
+    over = ((1,), (1,))
+
+    for tap, shift in enumerate(shifts):
+        patch_zero[tap * 8 : tap * 8 + 8] = pltpu.roll(layers[...], (-shift) % length, 1)
+
+    def spread(source):
+        for group in range(channels // 16):
+            rows = source[group * 16 : group * 16 + 16]
+            for tap, shift in enumerate(shifts):
+                high, low = halves(pltpu.roll(rows, (-shift) % length, 1))
+                start = tap * channels + group * 16
+                patch_high[start : start + 16] = high
+                patch_low[start : start + 16] = low
+
+    def each(body, init=0):
+        def step(index, carry):
+            return body(pl.ds(pl.multiple_of(index * chunk, chunk), chunk), carry)
+
+        return lax.fori_loop(0, pieces, step, init)
+
+    def slope(values):
+        squashed = 1.0 / (1.0 + jnp.exp(-values))
+        return squashed * (1.0 + values * (1.0 - squashed))
+
+    def silu(values):
+        return values / (1.0 + jnp.exp(-values))
+
+    def open_layer(at, carry):
+        high, low = halves(patch_zero[:, at])
+        both = dot3(first[...], high, low, flat)
+        inside = layers[4:5, at] > 0.5
+        before = both[:channels]
+        before_one[:, at] = before
+        hidden[:, at] = jnp.where(inside, silu(before), 0.0)
+        slope_two[:, at] = both[channels:]
+        return carry
+
+    each(open_layer)
+    spread(hidden)
+
+    def middle_layer(at, carry):
+        high = patch_high[:, at]
+        low = patch_low[:, at]
+        before = dot3(middle[...], high, low, flat)
+        inside = layers[4:5, at] > 0.5
+        owned = layers[5:6, at] > 0.5
+        after = jnp.where(inside, silu(before), 0.0)
+        hidden[:, at] = after
+        fall = jnp.where(inside, slope_two[:, at] * slope(before), 0.0)
+        slope_two[:, at] = fall
+        after_high, after_low = halves(after)
+        last_taps[:, at] = dot3(last[...], after_high, after_low, flat)
+        return carry + dot3(jnp.where(owned, fall, 0.0), high, low, over)
+
+    grad_middle = each(middle_layer, jnp.zeros((channels, 9 * channels), jnp.float32))
+    spread(slope_two)
+    update = layers[0:1]
+    for tap, shift in enumerate(shifts):
+        update = update + pltpu.roll(last_taps[...], (-shift) % length, 1)[tap : tap + 1]
+    new_velocity[...] = update
+
+    def first_grads(at, carry):
+        back = dot3(middle_back[...], patch_high[:, at], patch_low[:, at], flat)
+        owned = layers[5:6, at] > 0.5
+        fall = jnp.where(owned, back * slope(before_one[:, at]), 0.0)
+        high, low = halves(patch_zero[:, at])
+        return carry + dot3(jnp.concatenate([fall, hidden[:, at]], 0), high, low, over)
+
+    outer = each(first_grads, jnp.zeros((2 * channels, 72), jnp.float32))
+    grads[...] = jnp.zeros(grads.shape, jnp.float32)
+    grads[:, 0 : 9 * channels] = grad_middle
+    start = -(-9 * channels // 128) * 128
+    grads[:, start : start + 72] = outer[:channels]
+    grads[:, start + 128 : start + 200] = outer[channels:]
+
+
+def network(layers, width, conv_in, conv_mid, conv_out):
+    length = layers.shape[1]
+    channels = conv_mid.shape[0]
+    f32 = jnp.float32
+    taken = conv_in.reshape(channels, 9, 2)
+    first = jnp.concatenate(
+        [
+            jnp.pad(taken, ((0, 0), (0, 0), (0, 6))).reshape(channels, 72),
+            jnp.pad(flipped(conv_out)[:, :, None], ((0, 0), (0, 0), (2, 5))).reshape(channels, 72),
+        ],
+        0,
+    )
+    last = jnp.pad(conv_out.reshape(9, channels), ((0, 7), (0, 0)))
+    start = -(-9 * channels // 128) * 128
+    return pl.pallas_call(
+        functools.partial(network_kernel, width),
+        name="network",
+        out_shape=[
+            jax.ShapeDtypeStruct((1, length), f32),
+            jax.ShapeDtypeStruct((channels, start + 256), f32),
+        ],
+        in_specs=vmem(5),
+        out_specs=vmem(2),
+        scratch_shapes=[
+            pltpu.VMEM((72, length), f32),
+            pltpu.VMEM((9 * channels, length), jnp.bfloat16),
+            pltpu.VMEM((9 * channels, length), jnp.bfloat16),
+            pltpu.VMEM((channels, length), f32),
+            pltpu.VMEM((channels, length), f32),
+            pltpu.VMEM((channels, length), f32),
+            pltpu.VMEM((16, length), f32),
+        ],
+        compiler_params=pltpu.CompilerParams(vmem_limit_bytes=48 * 1024 * 1024),
+    )(first, conv_mid, flipped(conv_mid), last, layers)
+
+
+def update_model(imaging, velocity, cotangent, num_steps, shot_count, conv_in, conv_mid, conv_out):
+    rows, breadth = velocity.shape
+    piece = cotangent.shape[1]
+    channels = conv_mid.shape[0]
+    bands = lax.axis_size("band")
+    groups = lax.axis_size(group_axes)
+    image, cot, low, high = gather_pieces(imaging, velocity, cotangent)
+    scaled = image[5:-5, piece - 3 : 2 * piece + 3] / float(num_steps * shot_count) ** 0.5
+    cot = cot[5:-5, piece - 3 : 2 * piece + 3]
+    tall = jnp.concatenate([low[5:], velocity, high[:3]], 0)
+    start_col = lax.axis_index(group_axes) * piece
+    around = lax.dynamic_slice_in_dim(
+        jnp.pad(tall, ((0, 0), (piece, piece))), start_col, 3 * piece, 1
+    )[:, piece - 3 : 2 * piece + 3]
+    height, width = around.shape
+    row_ids = lax.axis_index("band") * rows - 3 + jnp.arange(height)
+    col_ids = start_col - 3 + jnp.arange(width)
+    inside = ((row_ids >= 0) & (row_ids < rows * bands))[:, None] & (
+        (col_ids >= 0) & (col_ids < piece * groups)
+    )[None, :]
+    owned = np.zeros((height, width), np.float32)
+    owned[3:-3, 3:-3] = 1.0
+    blank = jnp.zeros((height, width), jnp.float32)
+    layers = jnp.stack(
+        [around, scaled, cot, cot * owned, inside.astype(jnp.float32), jnp.asarray(owned), blank, blank]
+    ).reshape(8, height * width)
+    length = -(-height * width // chunk) * chunk
+    layers = jnp.pad(layers, ((0, 0), (0, length - height * width)))
+    fresh, grads = network(layers, width, conv_in, conv_mid, conv_out)
+    new_velocity = fresh[0, : height * width].reshape(height, width)[3:-3, 3:-3]
+    grads = total_grads(grads)
+    start = -(-9 * channels // 128) * 128
+    grad_in = grads[:, start : start + 72].reshape(channels, 9, 8)[:, :, :2].reshape(channels, 18)
+    spare = grads[:, start + 128 : start + 200].reshape(channels, 9, 8)[:, ::-1, 3]
+    return new_velocity, grad_in, grads[:, : 9 * channels], spare.T.reshape(1, 9 * channels)
 
 
 def on_device(
@@ -162,34 +599,9 @@
     adjoint = propagate(adjoint_last, adjoint_after, misfit[::-1], receiver_term)
     imaging = jnp.sum(stored * adjoint[::-1], axis=(0, 1))
     group_count = shot_here * lax.axis_size(("shot", "net"))
-    start_col = lax.axis_index(("shot", "net")) * piece_cols
-    gathered = lax.psum(imaging, ("shot", "net"))
-    summed = lax.dynamic_slice_in_dim(gathered, start_col, piece_cols, 1)
-    scaled = summed / float(num_steps * group_count) ** 0.5
-    velocity_piece = lax.dynamic_slice_in_dim(velocity, start_col, piece_cols, 1)
-
-    def spread(field):
-        extended = extended_2(field, (("band", 1), (("shot", "net"), 2)), 1)
-        return patches(extended, rows_here, piece_cols)
-
-    layer_zero = spread(jnp.stack([velocity_piece, scaled]))
-    before_one = matmul(conv_in, layer_zero)
-    hidden_one = jax.nn.silu(before_one)
-    layer_one = spread(hidden_one.reshape(-1, rows_here, piece_cols))
-    before_two = matmul(conv_mid, layer_one)
-    hidden_two = jax.nn.silu(before_two)
-    layer_two = spread(hidden_two.reshape(-1, rows_here, piece_cols))
-    update = matmul(conv_out, layer_two).reshape(rows_here, piece_cols)
-    new_velocity = velocity_piece + update
-    grad_out = outer_sum(cotangent.reshape(1, -1), layer_two)
-    slope_two = matmul(flipped(conv_out), spread(cotangent[None])) * sigmoid_slope(before_two)
-    grad_mid = outer_sum(slope_two, layer_one)
-    slope_one = matmul(
-        flipped(conv_mid), spread(slope_two.reshape(-1, rows_here, piece_cols))
-    ) * sigmoid_slope(before_one)
-    grad_in = outer_sum(slope_one, layer_zero)
-    totals = lax.psum((grad_in, grad_mid, grad_out), ("shot", "band", "net"))
-    return (new_velocity, totals[0], totals[1], totals[2])
+    return update_model(
+        imaging, velocity, cotangent, num_steps, group_count, conv_in, conv_mid, conv_out
+    )
 
 
 def solution(mesh):

time: 544 us -> 226 us (0.42); the launches traced: 534 us -> 225 us
  local copies, waits for them, and re-layouts: 169 us -> 36.7 us
  starting transfers between devices: 117 us -> 55.6 us
  waiting for transfers between devices: 76.8 us -> 15.9 us
  Pallas kernels: 0 us -> 47.4 us
  blocking collectives: 39.2 us -> 0 us
  other arithmetic: 78.2 us -> 49.7 us
  matrix products: 37.4 us -> 17.3 us
  between operations: 15.3 us -> 0.99 us
    slice x27 -> x10, local copies, waits for them, and re-layouts: 84.1 us -> 4.59 us  [the longest x2 1.52 us: update_model(): tall = jnp.concatenate([low[5:], velocity, high[:3]], 0)]
    psum x1 -> x0, waiting for transfers between devices: 55.1 us -> none  [on_device(): gathered = lax.psum(imaging, ('shot', 'net'))]
    ppermute x19 -> x9, starting transfers between devices: 91.8 us -> 44 us  [extended_2(): lax.ppermute(lax.slice_in_dim(block, block.shape[dim] - width, None, axis...]
    pallas_call x0 -> x3, Pallas kernels: none -> 47.4 us  [the longest x1 17.4 us: total_grads(): pl.pallas_call(functools.partial(total_kernel, sizes), name='total_grads'...]
    psum x1 -> x0, blocking collectives: 39.2 us -> none  [on_device(): totals = lax.psum((grad_in, grad_mid, grad_out), ('shot', 'band', 'net'))]
    concatenate x23 -> x9, other arithmetic: 27.2 us -> 0.58 us  [extended_2(): block = jnp.concatenate([low, block, high], axis=dim)]
    unnamed x126 -> x26, local copies, waits for them, and re-layouts: 22.8 us -> 2.34 us
    ppermute x6 -> x0, local copies, waits for them, and re-layouts: 20.1 us -> none  [the longest x3 10.7 us: extended_2(): lax.ppermute(lax.slice_in_dim(block, block.shape[dim] - width, None, axis...]
  transfers between devices with their start and end apart: 39 -> 18, of which waited for: 11 -> 8; matrix products, arithmetic and copies ran while one was open for 28% -> 11% of each run, Pallas kernels for 0% -> 0%
where the time goes in v1:
time: 226 us; the launch traced here: 225 us
  starting transfers between devices  55.6 us (25%)
  other arithmetic  49.7 us (22%)
  Pallas kernels  47.4 us (21%)
  local copies, waits for them, and re-layouts  36.7 us (16%)
  matrix products  17.3 us (8%)
  waiting for transfers between devices  15.9 us (7%)
    ppermute x9, starting transfers between devices, extended_2(): lax.ppermute(lax.slice_in_dim(block, block.shape[dim] - width, None, axis...  44 us
    add x24, other arithmetic, block(): 2.0 * current[:, 4:-4] - earlier[:, 4:-4] + speed_part * laplace(current)  21.6 us
    pallas_call x1, Pallas kernels, total_grads(): pl.pallas_call(functools.partial(total_kernel, sizes), name='total_grads'...  17.4 us
    dot_general x16, matrix products, receiver_term(): injected = jnp.einsum('swk,sk->sw', table, residual, precision=highest)  16.8 us
    pallas_call x1, Pallas kernels, network(): pl.pallas_call(functools.partial(network_kernel, width), name='network',...  15.5 us
    pallas_call x1, Pallas kernels, gather_pieces(): pl.pallas_call(functools.partial(gather_kernel, groups, nets, bands), nam...  14.5 us
    ppermute x9, starting transfers between devices, extended_2(): lax.ppermute(lax.slice_in_dim(block, 0, width, axis=dim), axis, backward)  11.6 us
    reshape x2, local copies, waits for them, and re-layouts, propagate(): return states.reshape((num_steps,) + start.shape)  11.2 us
  transfers between devices with their start and end apart: 18, of which 8 were waited for; matrix products, arithmetic and copies ran while one was open for 11% of the time, Pallas kernels for 0%

profile of v1, /device:TPU:0, one launch (start us, length us, event | category | flops | bytes accessed | tf_op | source)
XLA Modules:
  0.0 225.1 jit_solution(3251882293626447012)
XLA Ops:
  1.7 5.0 %collective-permute-start.4 = (f32[16,1024]{1,0:T(8,128)S(1)}, f32[16,1024]{1,0:T(8,128)S(1)}, u32[]{:S(2)}, u32[]{:S(2)}) collective-permute-start(f32[16,1024]{1,0:T(8,128)S(1)} %get-tuple-element.455), channel_id=1, source_target_pairs={{0,2},{2,4},{4,6},{1,3},{3,5},{5,7},{8,10},{10,12},{12,14},{9,11},... | collective-permute-start | bytes 196616 | tf_op jit(solution)/shard_map/ppermute | solution.py:23
  6.6 1.3 collective-permute-start.5
  15.1 2.5 %broadcast.587.clone = f32[4,4,2,32,1024]{4,3,2,1,0:T(8,128)} broadcast(f32[]{:T(128)} %constant.216.clone.1), dimensions={} | broadcast | bytes 4194308 | tf_op jit(solution)/shard_map/broadcast.114
  17.6 62.0 %while.34 = (s32[]{:T(128)}, f32[2,32,1024]{2,1,0:T(8,128)S(1)}, f32[2,32,1024]{2,1,0:T(8,128)S(1)}, f32[4,4,2,32,1024]{4,3,2,1,0:T(8,128)}, f32[64,1024]{1,0:T(...) while((s32[]{:T(128)}, f32[2,32,1024]{2,1,0:T(8,128)S(1)}, ...), condition=%wide.region_1.2_spmd.clone, body=%wide.region_0.1_spmd.clone.sunk | while | flops 11801106 | bytes 31434516 | solution.py:593
  17.7 1.3 collective-permute-start
  19.0 5.2 %collective-permute-start.1 = (f32[2,2,16,1024]{3,2,1,0:T(8,128)S(1)}, f32[2,2,16,1024]{3,2,1,0:T(8,128)S(1)}, u32[]{:S(2)}, u32[]{:S(2)}) collective-permute-start(f32[2,2,16,1024]{3,2,1,0:T(8,128)S(1)} %get-tuple-element.622), channel_id=1, source_target_pairs={{0,2},{2,4},{4,6},{1,3},{3,5},{5,7},{8,10},{10,12},{12,14},{9,11},... | collective-permute-start | bytes 786440 | tf_op jit(solution)/shard_map/while/body/eval_jaxpr/ppermute | solution.py:23
  24.4 3.6 %collective-permute-done = f32[2,2,16,1024]{3,2,1,0:T(8,128)S(1)} collective-permute-done((f32[2,2,16,1024]{3,2,1,0:T(8,128)S(1)}, f32[2,2,16,1024]{3,2,1,0:T(8,128)S(1)}, u32[]{:S(2)}, u32[]{:S(2)}) %collective-permute-start) | collective-permute-done | bytes 262176 | tf_op jit(solution)/shard_map/while/body/eval_jaxpr/ppermute | solution.py:26
  28.0 1.2 collective-permute-done.1
  29.4 1.0 fusion.234
  32.9 1.2 fusion.237
  34.1 1.3 collective-permute-start
  35.4 5.0 %collective-permute-start.1 = (f32[2,2,16,1024]{3,2,1,0:T(8,128)S(1)}, f32[2,2,16,1024]{3,2,1,0:T(8,128)S(1)}, u32[]{:S(2)}, u32[]{:S(2)}) collective-permute-start(f32[2,2,16,1024]{3,2,1,0:T(8,128)S(1)} %get-tuple-element.622), channel_id=1, source_target_pairs={{0,2},{2,4},{4,6},{1,3},{3,5},{5,7},{8,10},{10,12},{12,14},{9,11},... | collective-permute-start | bytes 786440 | tf_op jit(solution)/shard_map/while/body/eval_jaxpr/ppermute | solution.py:23
  40.7 2.7 %collective-permute-done = f32[2,2,16,1024]{3,2,1,0:T(8,128)S(1)} collective-permute-done((f32[2,2,16,1024]{3,2,1,0:T(8,128)S(1)}, f32[2,2,16,1024]{3,2,1,0:T(8,128)S(1)}, u32[]{:S(2)}, u32[]{:S(2)}) %collective-permute-start) | collective-permute-done | bytes 262176 | tf_op jit(solution)/shard_map/while/body/eval_jaxpr/ppermute | solution.py:26
  43.4 1.2 collective-permute-done.1
  44.8 1.0 fusion.234
  48.3 1.1 fusion.237
  49.5 1.3 collective-permute-start
  50.8 5.0 %collective-permute-start.1 = (f32[2,2,16,1024]{3,2,1,0:T(8,128)S(1)}, f32[2,2,16,1024]{3,2,1,0:T(8,128)S(1)}, u32[]{:S(2)}, u32[]{:S(2)}) collective-permute-start(f32[2,2,16,1024]{3,2,1,0:T(8,128)S(1)} %get-tuple-element.622), channel_id=1, source_target_pairs={{0,2},{2,4},{4,6},{1,3},{3,5},{5,7},{8,10},{10,12},{12,14},{9,11},... | collective-permute-start | bytes 786440 | tf_op jit(solution)/shard_map/while/body/eval_jaxpr/ppermute | solution.py:23
  56.0 2.2 collective-permute-done
  58.2 1.5 collective-permute-done.1
  59.9 1.0 fusion.234
  63.4 1.1 fusion.237
  64.5 1.3 collective-permute-start
  65.8 5.0 %collective-permute-start.1 = (f32[2,2,16,1024]{3,2,1,0:T(8,128)S(1)}, f32[2,2,16,1024]{3,2,1,0:T(8,128)S(1)}, u32[]{:S(2)}, u32[]{:S(2)}) collective-permute-start(f32[2,2,16,1024]{3,2,1,0:T(8,128)S(1)} %get-tuple-element.622), channel_id=1, source_target_pairs={{0,2},{2,4},{4,6},{1,3},{3,5},{5,7},{8,10},{10,12},{12,14},{9,11},... | collective-permute-start | bytes 786440 | tf_op jit(solution)/shard_map/while/body/eval_jaxpr/ppermute | solution.py:23
  71.1 2.2 collective-permute-done
  73.3 1.5 collective-permute-done.1
  75.0 1.0 fusion.234
  78.5 1.1 fusion.237
  79.6 4.6 %copy.50 = f32[16,2,32,1024]{3,0,1,2:T(8,128)S(1)} copy(f32[16,2,32,1024]{3,2,1,0:T(8,128)} %bitcast.192) | data formatting | bytes 8388608 | tf_op jit(solution)/shard_map/reshape | solution.py:594
  84.8 2.5 %broadcast.587 = f32[4,4,2,32,1024]{4,3,2,1,0:T(8,128)} broadcast(f32[]{:T(128)} %constant.216.clone.1), dimensions={} | broadcast | bytes 4194308 | tf_op jit(solution)/shard_map/broadcast.114
  87.3 61.2 %while.35 = (s32[]{:T(128)}, f32[2,32,1024]{2,1,0:T(8,128)S(1)}, f32[2,32,1024]{2,1,0:T(8,128)S(1)}, f32[4,4,2,32,1024]{4,3,2,1,0:T(8,128)}, f32[64,1024]{1,0:T(...) while((s32[]{:T(128)}, f32[2,32,1024]{2,1,0:T(8,128)S(1)}, ...), condition=%wide.region_3.4_spmd.clone, body=%wide.region_2.3_spmd.clone.sunk | while | flops 27165204 | bytes 31534800 | solution.py:593
  87.3 1.3 collective-permute-start.2
  88.6 5.0 %collective-permute-start.3 = (f32[2,2,16,1024]{3,2,1,0:T(8,128)S(1)}, f32[2,2,16,1024]{3,2,1,0:T(8,128)S(1)}, u32[]{:S(2)}, u32[]{:S(2)}) collective-permute-start(f32[2,2,16,1024]{3,2,1,0:T(8,128)S(1)} %get-tuple-element.645), channel_id=1, source_target_pairs={{0,2},{2,4},{4,6},{1,3},{3,5},{5,7},{8,10},{10,12},{12,14},{9,11},... | collective-permute-start | bytes 786440 | tf_op jit(solution)/shard_map/while/body/eval_jaxpr/ppermute | solution.py:23
  93.7 1.0 fusion.247
  94.7 1.1 fusion.249
  95.8 1.1 fusion.252
  96.8 1.1 fusion.251
  101.8 1.1 fusion.254
  103.0 1.3 collective-permute-start.2
  104.3 4.6 %collective-permute-start.3 = (f32[2,2,16,1024]{3,2,1,0:T(8,128)S(1)}, f32[2,2,16,1024]{3,2,1,0:T(8,128)S(1)}, u32[]{:S(2)}, u32[]{:S(2)}) collective-permute-start(f32[2,2,16,1024]{3,2,1,0:T(8,128)S(1)} %get-tuple-element.645), channel_id=1, source_target_pairs={{0,2},{2,4},{4,6},{1,3},{3,5},{5,7},{8,10},{10,12},{12,14},{9,11},... | collective-permute-start | bytes 786440 | tf_op jit(solution)/shard_map/while/body/eval_jaxpr/ppermute | solution.py:23
  108.9 1.0 fusion.247
  109.9 1.1 fusion.249
  111.0 1.1 fusion.252
  112.0 1.1 fusion.251
  117.0 1.1 fusion.254
  118.1 1.3 collective-permute-start.2
  119.4 4.6 %collective-permute-start.3 = (f32[2,2,16,1024]{3,2,1,0:T(8,128)S(1)}, f32[2,2,16,1024]{3,2,1,0:T(8,128)S(1)}, u32[]{:S(2)}, u32[]{:S(2)}) collective-permute-start(f32[2,2,16,1024]{3,2,1,0:T(8,128)S(1)} %get-tuple-element.645), channel_id=1, source_target_pairs={{0,2},{2,4},{4,6},{1,3},{3,5},{5,7},{8,10},{10,12},{12,14},{9,11},... | collective-permute-start | bytes 786440 | tf_op jit(solution)/shard_map/while/body/eval_jaxpr/ppermute | solution.py:23
  125.1 1.1 fusion.249
  126.1 1.1 fusion.252
  127.2 1.1 fusion.251
  132.2 1.1 fusion.254
  133.3 1.3 collective-permute-start.2
  134.6 4.6 %collective-permute-start.3 = (f32[2,2,16,1024]{3,2,1,0:T(8,128)S(1)}, f32[2,2,16,1024]{3,2,1,0:T(8,128)S(1)}, u32[]{:S(2)}, u32[]{:S(2)}) collective-permute-start(f32[2,2,16,1024]{3,2,1,0:T(8,128)S(1)} %get-tuple-element.645), channel_id=1, source_target_pairs={{0,2},{2,4},{4,6},{1,3},{3,5},{5,7},{8,10},{10,12},{12,14},{9,11},... | collective-permute-start | bytes 786440 | tf_op jit(solution)/shard_map/while/body/eval_jaxpr/ppermute | solution.py:23
  140.3 1.1 fusion.249
  141.3 1.1 fusion.252
  142.4 1.1 fusion.251
  147.4 1.1 fusion.254
  148.5 6.6 %copy.51 = f32[16,2,32,1024]{3,0,1,2:T(8,128)} copy(f32[16,2,32,1024]{3,2,1,0:T(8,128)} %bitcast.194) | data formatting | bytes 8388608 | tf_op jit(solution)/shard_map/reshape | solution.py:594
  155.1 6.7 %rev.18 = f32[16,2,32,1024]{3,0,1,2:T(8,128)} reverse(f32[16,2,32,1024]{3,0,1,2:T(8,128)} %copy.51), dimensions={0} | reverse | bytes 8388608 | tf_op jit(solution)/shard_map/rev | solution.py:600
  161.8 7.1 %multiply_reduce_fusion.image = f32[32,1024]{1,0:T(8,128)} fusion(f32[16,2,32,1024]{3,0,1,2:T(8,128)} %rev.18, f32[16,2,32,1024]{3,2,1,0:T(8,128)} %bitcast.193), kind=kLoop, calls=%fused_computation.323 | loop fusion | flops 2064384 | bytes 8519680 | tf_op jit(solution)/shard_map/reduce_sum | solution.py:600
  168.9 14.5 %gather_pieces.1 = (f32[48,384]{1,0:T(8,128)}, f32[48,384]{1,0:T(8,128)}, f32[8,1024]{1,0:T(8,128)}, f32[8,1024]{1,0:T(8,128)}) custom-call(f32[32,1024]{1,0:T(8,128)} %multiply_reduce_fusion.image, f32[32,1024]{1,0:T(8,128)} %velocity.1, f32[32,128]{1,0:T(8,128)} %cotangent.1), custom_call_target="tpu_custom_call" | custom-call | tf_op jit(solution)/shard_map/gather_pieces/pallas_call | solution.py:228
  187.0 15.5 %network.1 = (f32[1,5120]{1,0:T(1,128)S(1)}, f32[32,640]{1,0:T(8,128)S(1)}) custom-call(f32[64,72]{1,0:T(8,128)S(1)} %pad_maximum_fusion.5.first, f32[32,288]{1,0:T(8,128)S(1)} %copy-done, f32[32,288]{1,0:T(8,128)S(1)} %copy.38.middle_back, f32[16,32]{1,0:T(8,128)S(1)} %pad.74.last, f32[8,5120]{1,0:T(8,128)S(1)} %pad.76.layers), custom_call_target="tpu_custom_call" | custom-call | tf_op jit(solution)/shard_map/network/pallas_call | solution.py:467
  203.2 17.4 %total_grads.1 = f32[32,640]{1,0:T(8,128)} custom-call(f32[32,640]{1,0:T(8,128)} %copy-done.1), custom_call_target="tpu_custom_call" | custom-call | tf_op jit(solution)/shard_map/total_grads/pallas_call | solution.py:331
  221.3 1.4 slice.1101
  (274 shorter events, 44.6 us)
Async XLA Ops:
  0.6 17.0 %copy-start.3 = (f32[2,32,1024]{2,1,0:T(8,128)S(1)}, f32[2,32,1024]{2,1,0:T(8,128)}, u32[]{:S(2)}) copy-start(f32[2,32,1024]{2,1,0:T(8,128)} %param.21) | copy-start | bytes 786436
  0.6 17.0 %copy-start.4 = (f32[2,32,1024]{2,1,0:T(8,128)S(1)}, f32[2,32,1024]{2,1,0:T(8,128)}, u32[]{:S(2)}) copy-start(f32[2,32,1024]{2,1,0:T(8,128)} %param.22) | copy-start | bytes 786436
  0.7 17.0 %copy-start.9 = (s32[2]{0:T(128)S(1)}, s32[2]{0:T(128)}, u32[]{:S(2)}) copy-start(s32[2]{0:T(128)} %param.26) | copy-start | bytes 28
  1.7 13.4 %collective-permute-start.4 = (f32[16,1024]{1,0:T(8,128)S(1)}, f32[16,1024]{1,0:T(8,128)S(1)}, u32[]{:S(2)}, u32[]{:S(2)}) collective-permute-start(f32[16,1024]{1,0:T(8,128)S(1)} %get-tuple-element.455), channel_id=1, source_target_pairs={{0,2},{2,4},{4,6},{1,3},{3,5},{5,7},{8,10},{10,12},{12,14},{9,11},... | collective-permute-start | bytes 196616 | tf_op jit(solution)/shard_map/ppermute | solution.py:23
  6.6 8.4 %collective-permute-start.5 = (f32[16,1024]{1,0:T(8,128)S(1)}, f32[16,1024]{1,0:T(8,128)S(1)}, u32[]{:S(2)}, u32[]{:S(2)}) collective-permute-start(f32[16,1024]{1,0:T(8,128)S(1)} %get-tuple-element.456), channel_id=1, source_target_pairs={{2,0},{4,2},{6,4},{3,1},{5,3},{7,5},{10,8},{12,10},{14,12},{11,9},... | collective-permute-start | bytes 196616 | tf_op jit(solution)/shard_map/ppermute | solution.py:26
  17.7 10.3 %collective-permute-start = (f32[2,2,16,1024]{3,2,1,0:T(8,128)S(1)}, f32[2,2,16,1024]{3,2,1,0:T(8,128)S(1)}, u32[]{:S(2)}, u32[]{:S(2)}) collective-permute-start(f32[2,2,16,1024]{3,2,1,0:T(8,128)S(1)} %get-tuple-element.621), channel_id=1, source_target_pairs={{2,0},{4,2},{6,4},{3,1},{5,3},{7,5},{10,8},{12,10},{14,12},{11,9},... | collective-permute-start | bytes 786440 | tf_op jit(solution)/shard_map/while/body/eval_jaxpr/ppermute | solution.py:26
  19.0 10.2 %collective-permute-start.1 = (f32[2,2,16,1024]{3,2,1,0:T(8,128)S(1)}, f32[2,2,16,1024]{3,2,1,0:T(8,128)S(1)}, u32[]{:S(2)}, u32[]{:S(2)}) collective-permute-start(f32[2,2,16,1024]{3,2,1,0:T(8,128)S(1)} %get-tuple-element.622), channel_id=1, source_target_pairs={{0,2},{2,4},{4,6},{1,3},{3,5},{5,7},{8,10},{10,12},{12,14},{9,11},... | collective-permute-start | bytes 786440 | tf_op jit(solution)/shard_map/while/body/eval_jaxpr/ppermute | solution.py:23
  34.1 9.3 %collective-permute-start = (f32[2,2,16,1024]{3,2,1,0:T(8,128)S(1)}, f32[2,2,16,1024]{3,2,1,0:T(8,128)S(1)}, u32[]{:S(2)}, u32[]{:S(2)}) collective-permute-start(f32[2,2,16,1024]{3,2,1,0:T(8,128)S(1)} %get-tuple-element.621), channel_id=1, source_target_pairs={{2,0},{4,2},{6,4},{3,1},{5,3},{7,5},{10,8},{12,10},{14,12},{11,9},... | collective-permute-start | bytes 786440 | tf_op jit(solution)/shard_map/while/body/eval_jaxpr/ppermute | solution.py:26
  35.4 9.1 %collective-permute-start.1 = (f32[2,2,16,1024]{3,2,1,0:T(8,128)S(1)}, f32[2,2,16,1024]{3,2,1,0:T(8,128)S(1)}, u32[]{:S(2)}, u32[]{:S(2)}) collective-permute-start(f32[2,2,16,1024]{3,2,1,0:T(8,128)S(1)} %get-tuple-element.622), channel_id=1, source_target_pairs={{0,2},{2,4},{4,6},{1,3},{3,5},{5,7},{8,10},{10,12},{12,14},{9,11},... | collective-permute-start | bytes 786440 | tf_op jit(solution)/shard_map/while/body/eval_jaxpr/ppermute | solution.py:23
  49.5 8.7 %collective-permute-start = (f32[2,2,16,1024]{3,2,1,0:T(8,128)S(1)}, f32[2,2,16,1024]{3,2,1,0:T(8,128)S(1)}, u32[]{:S(2)}, u32[]{:S(2)}) collective-permute-start(f32[2,2,16,1024]{3,2,1,0:T(8,128)S(1)} %get-tuple-element.621), channel_id=1, source_target_pairs={{2,0},{4,2},{6,4},{3,1},{5,3},{7,5},{10,8},{12,10},{14,12},{11,9},... | collective-permute-start | bytes 786440 | tf_op jit(solution)/shard_map/while/body/eval_jaxpr/ppermute | solution.py:26
  50.8 8.9 %collective-permute-start.1 = (f32[2,2,16,1024]{3,2,1,0:T(8,128)S(1)}, f32[2,2,16,1024]{3,2,1,0:T(8,128)S(1)}, u32[]{:S(2)}, u32[]{:S(2)}) collective-permute-start(f32[2,2,16,1024]{3,2,1,0:T(8,128)S(1)} %get-tuple-element.622), channel_id=1, source_target_pairs={{0,2},{2,4},{4,6},{1,3},{3,5},{5,7},{8,10},{10,12},{12,14},{9,11},... | collective-permute-start | bytes 786440 | tf_op jit(solution)/shard_map/while/body/eval_jaxpr/ppermute | solution.py:23
  64.5 8.7 %collective-permute-start = (f32[2,2,16,1024]{3,2,1,0:T(8,128)S(1)}, f32[2,2,16,1024]{3,2,1,0:T(8,128)S(1)}, u32[]{:S(2)}, u32[]{:S(2)}) collective-permute-start(f32[2,2,16,1024]{3,2,1,0:T(8,128)S(1)} %get-tuple-element.621), channel_id=1, source_target_pairs={{2,0},{4,2},{6,4},{3,1},{5,3},{7,5},{10,8},{12,10},{14,12},{11,9},... | collective-permute-start | bytes 786440 | tf_op jit(solution)/shard_map/while/body/eval_jaxpr/ppermute | solution.py:26
  65.8 8.9 %collective-permute-start.1 = (f32[2,2,16,1024]{3,2,1,0:T(8,128)S(1)}, f32[2,2,16,1024]{3,2,1,0:T(8,128)S(1)}, u32[]{:S(2)}, u32[]{:S(2)}) collective-permute-start(f32[2,2,16,1024]{3,2,1,0:T(8,128)S(1)} %get-tuple-element.622), channel_id=1, source_target_pairs={{0,2},{2,4},{4,6},{1,3},{3,5},{5,7},{8,10},{10,12},{12,14},{9,11},... | collective-permute-start | bytes 786440 | tf_op jit(solution)/shard_map/while/body/eval_jaxpr/ppermute | solution.py:23
  79.6 4.7 %copy-start.10 = (f32[2,16,128]{2,1,0:T(8,128)S(1)}, f32[2,16,128]{2,1,0:T(8,128)}, u32[]{:S(2)}) copy-start(f32[2,16,128]{2,1,0:T(8,128)} %param.30) | copy-start | bytes 49156
  84.2 3.0 %copy-start.2 = (f32[2,32,1024]{2,1,0:T(8,128)S(1)}, f32[2,32,1024]{2,1,0:T(8,128)}, u32[]{:S(2)}) copy-start(f32[2,32,1024]{2,1,0:T(8,128)} %param.23) | copy-start | bytes 786436
  84.3 3.0 %copy-start.5 = (f32[2,32,1024]{2,1,0:T(8,128)S(1)}, f32[2,32,1024]{2,1,0:T(8,128)}, u32[]{:S(2)}) copy-start(f32[2,32,1024]{2,1,0:T(8,128)} %param.24) | copy-start | bytes 786436
  87.3 10.7 %collective-permute-start.2 = (f32[2,2,16,1024]{3,2,1,0:T(8,128)S(1)}, f32[2,2,16,1024]{3,2,1,0:T(8,128)S(1)}, u32[]{:S(2)}, u32[]{:S(2)}) collective-permute-start(f32[2,2,16,1024]{3,2,1,0:T(8,128)S(1)} %get-tuple-element.644), channel_id=1, source_target_pairs={{2,0},{4,2},{6,4},{3,1},{5,3},{7,5},{10,8},{12,10},{14,12},{11,9},... | collective-permute-start | bytes 786440 | tf_op jit(solution)/shard_map/while/body/eval_jaxpr/ppermute | solution.py:26
  88.6 9.5 %collective-permute-start.3 = (f32[2,2,16,1024]{3,2,1,0:T(8,128)S(1)}, f32[2,2,16,1024]{3,2,1,0:T(8,128)S(1)}, u32[]{:S(2)}, u32[]{:S(2)}) collective-permute-start(f32[2,2,16,1024]{3,2,1,0:T(8,128)S(1)} %get-tuple-element.645), channel_id=1, source_target_pairs={{0,2},{2,4},{4,6},{1,3},{3,5},{5,7},{8,10},{10,12},{12,14},{9,11},... | collective-permute-start | bytes 786440 | tf_op jit(solution)/shard_map/while/body/eval_jaxpr/ppermute | solution.py:23
  103.0 10.3 %collective-permute-start.2 = (f32[2,2,16,1024]{3,2,1,0:T(8,128)S(1)}, f32[2,2,16,1024]{3,2,1,0:T(8,128)S(1)}, u32[]{:S(2)}, u32[]{:S(2)}) collective-permute-start(f32[2,2,16,1024]{3,2,1,0:T(8,128)S(1)} %get-tuple-element.644), channel_id=1, source_target_pairs={{2,0},{4,2},{6,4},{3,1},{5,3},{7,5},{10,8},{12,10},{14,12},{11,9},... | collective-permute-start | bytes 786440 | tf_op jit(solution)/shard_map/while/body/eval_jaxpr/ppermute | solution.py:26
  104.3 9.0 %collective-permute-start.3 = (f32[2,2,16,1024]{3,2,1,0:T(8,128)S(1)}, f32[2,2,16,1024]{3,2,1,0:T(8,128)S(1)}, u32[]{:S(2)}, u32[]{:S(2)}) collective-permute-start(f32[2,2,16,1024]{3,2,1,0:T(8,128)S(1)} %get-tuple-element.645), channel_id=1, source_target_pairs={{0,2},{2,4},{4,6},{1,3},{3,5},{5,7},{8,10},{10,12},{12,14},{9,11},... | collective-permute-start | bytes 786440 | tf_op jit(solution)/shard_map/while/body/eval_jaxpr/ppermute | solution.py:23
  118.1 10.3 %collective-permute-start.2 = (f32[2,2,16,1024]{3,2,1,0:T(8,128)S(1)}, f32[2,2,16,1024]{3,2,1,0:T(8,128)S(1)}, u32[]{:S(2)}, u32[]{:S(2)}) collective-permute-start(f32[2,2,16,1024]{3,2,1,0:T(8,128)S(1)} %get-tuple-element.644), channel_id=1, source_target_pairs={{2,0},{4,2},{6,4},{3,1},{5,3},{7,5},{10,8},{12,10},{14,12},{11,9},... | collective-permute-start | bytes 786440 | tf_op jit(solution)/shard_map/while/body/eval_jaxpr/ppermute | solution.py:26
  119.4 9.0 %collective-permute-start.3 = (f32[2,2,16,1024]{3,2,1,0:T(8,128)S(1)}, f32[2,2,16,1024]{3,2,1,0:T(8,128)S(1)}, u32[]{:S(2)}, u32[]{:S(2)}) collective-permute-start(f32[2,2,16,1024]{3,2,1,0:T(8,128)S(1)} %get-tuple-element.645), channel_id=1, source_target_pairs={{0,2},{2,4},{4,6},{1,3},{3,5},{5,7},{8,10},{10,12},{12,14},{9,11},... | collective-permute-start | bytes 786440 | tf_op jit(solution)/shard_map/while/body/eval_jaxpr/ppermute | solution.py:23
  133.3 10.3 %collective-permute-start.2 = (f32[2,2,16,1024]{3,2,1,0:T(8,128)S(1)}, f32[2,2,16,1024]{3,2,1,0:T(8,128)S(1)}, u32[]{:S(2)}, u32[]{:S(2)}) collective-permute-start(f32[2,2,16,1024]{3,2,1,0:T(8,128)S(1)} %get-tuple-element.644), channel_id=1, source_target_pairs={{2,0},{4,2},{6,4},{3,1},{5,3},{7,5},{10,8},{12,10},{14,12},{11,9},... | collective-permute-start | bytes 786440 | tf_op jit(solution)/shard_map/while/body/eval_jaxpr/ppermute | solution.py:26
  134.6 9.0 %collective-permute-start.3 = (f32[2,2,16,1024]{3,2,1,0:T(8,128)S(1)}, f32[2,2,16,1024]{3,2,1,0:T(8,128)S(1)}, u32[]{:S(2)}, u32[]{:S(2)}) collective-permute-start(f32[2,2,16,1024]{3,2,1,0:T(8,128)S(1)} %get-tuple-element.645), channel_id=1, source_target_pairs={{0,2},{2,4},{4,6},{1,3},{3,5},{5,7},{8,10},{10,12},{12,14},{9,11},... | collective-permute-start | bytes 786440 | tf_op jit(solution)/shard_map/while/body/eval_jaxpr/ppermute | solution.py:23
  161.8 21.6 %copy-start.7 = (f32[38,134]{1,0:T(8,128)S(1)}, f32[38,134]{1,0:T(8,128)}, u32[]{:S(2)}) copy-start(f32[38,134]{1,0:T(8,128)} %constant.232.clone) | copy-start | bytes 61108
  161.8 24.7 %copy-start.6 = (f32[32,1024]{1,0:T(8,128)S(1)}, f32[32,1024]{1,0:T(8,128)}, u32[]{:S(2)}) copy-start(f32[32,1024]{1,0:T(8,128)} %velocity.1) | copy-start | bytes 393220
  161.8 25.0 %copy-start.8 = (f32[1,5092]{1,0:T(1,128)S(1)}, f32[1,5092]{1,0:T(1,128)}, u32[]{:S(2)}) copy-start(f32[1,5092]{1,0:T(1,128)} %constant.269) | copy-start | bytes 61108
  161.8 25.2 %copy-start = (f32[32,288]{1,0:T(8,128)S(1)}, f32[32,288]{1,0:T(8,128)}, u32[]{:S(2)}) copy-start(f32[32,288]{1,0:T(8,128)} %middle.1) | copy-start | bytes 110596
  202.6 0.6 copy-start.1

commit v2 on v1

--- a/solution.py
+++ b/solution.py
@@ -13,39 +13,6 @@
 source_depth = 2
 receiver_depth = 3
 highest = lax.Precision.HIGHEST
-
-
-def extended_2(block, sides, width):
-    for axis, dim in sides:
-        count = lax.axis_size(axis)
-        forward = [(i, i + 1) for i in range(count - 1)]
-        backward = [(target, source) for source, target in forward]
-        low = lax.ppermute(
-            lax.slice_in_dim(block, block.shape[dim] - width, None, axis=dim), axis, forward
-        )
-        high = lax.ppermute(lax.slice_in_dim(block, 0, width, axis=dim), axis, backward)
-        block = jnp.concatenate([low, block, high], axis=dim)
-    return block
-
-
-def laplace(extended):
-    middle = extended[..., 4:-4, :]
-    height = middle.shape[-2]
-    breadth = middle.shape[-1]
-    padding = [(0, 0)] * (middle.ndim - 1) + [(4, 4)]
-    padded = jnp.pad(middle, padding)
-    running = 2.0 * coefficients[0] * middle
-    for reach in range(1, 5):
-        vertical = (
-            extended[..., 4 - reach : 4 - reach + height, :]
-            + extended[..., 4 + reach : 4 + reach + height, :]
-        )
-        lateral = (
-            padded[..., 4 - reach : 4 - reach + breadth]
-            + padded[..., 4 + reach : 4 + reach + breadth]
-        )
-        running = running + coefficients[reach] * (vertical + lateral)
-    return running
 
 
 def receiver_table(rec_first, rec_last, rec_count, breadth, slots):
@@ -344,6 +311,308 @@
         ],
         compiler_params=pltpu.CompilerParams(collective_id=2, has_side_effects=True),
     )(grads)
+
+
+lead = 16
+
+
+def advance(now, prior, speed):
+    middle = now(0)
+    wide = jnp.concatenate([middle, jnp.zeros((middle.shape[0], 128), jnp.float32)], 1)
+    breadth = middle.shape[1]
+    running = 2.0 * coefficients[0] * middle
+    for reach in range(1, 5):
+        lateral = pltpu.roll(wide, reach, 1) + pltpu.roll(wide, breadth + 128 - reach, 1)
+        running = running + coefficients[reach] * (
+            now(-reach) + now(reach) + lateral[:, :breadth]
+        )
+    return 2.0 * middle - prior + speed * running
+
+
+def wave_kernel(
+    bands, near_bands,
+    velocity, wave_now, wave_before, adjoint_last, adjoint_after, drive, marked, recorded,
+    image,
+    states, speeds, near_speed, bursts, injected,
+    send, receive, speed_send, speed_receive, near_send, near_receive, burst_send, burst_receive,
+):
+    shots, rows, breadth = wave_now.shape
+    steps = drive.shape[0]
+    pairs = steps // 2
+    band = lax.axis_index("band")
+    tall = rows + 2 * lead
+    margin = 8
+    upper = pl.ds(lead - 8, 8)
+    lower = pl.ds(lead + rows, 8)
+    own = pl.ds(lead, rows)
+    low_near = lax.min(lax.max(near_bands - band, 0), 1)
+
+    @pl.when(band == 0)
+    def _():
+        for field in range(2):
+            for shot in range(shots):
+                states[field, 0, shot, upper] = jnp.zeros((8, breadth), jnp.float32)
+                for slot in range(1, steps + 2, 2):
+                    states[field, slot, shot, upper] = jnp.zeros((8, breadth), jnp.float32)
+        speeds[upper] = jnp.zeros((8, breadth), jnp.float32)
+
+    @pl.when(band == bands - 1)
+    def _():
+        for field in range(2):
+            for shot in range(shots):
+                states[field, 0, shot, lower] = jnp.zeros((8, breadth), jnp.float32)
+                for slot in range(1, steps + 2, 2):
+                    states[field, slot, shot, lower] = jnp.zeros((8, breadth), jnp.float32)
+        speeds[lower] = jnp.zeros((8, breadth), jnp.float32)
+
+    barrier = pltpu.get_barrier_semaphore()
+
+    def meet(offset):
+        pl.semaphore_signal(
+            barrier, inc=1, device_id={"band": band + offset}, device_id_type=MESH
+        )
+
+    pl.when(band > 0)(lambda: meet(-1))
+    pl.when(band < bands - 1)(lambda: meet(1))
+    count = lax.min(band, 1) + lax.min(bands - 1 - band, 1)
+    for offset in range(2, near_bands):
+        pl.when(band + offset < near_bands)(lambda: meet(offset))
+        pl.when((band < near_bands) & (band >= offset))(lambda: meet(-offset))
+        count = count + lax.min(lax.max(near_bands - offset - band, 0), 1)
+        count = count + low_near * lax.min(lax.max(band - offset + 1, 0), 1)
+    pl.semaphore_wait(barrier, count)
+
+    def sides(source_up, source_down, target_up, target_down, sends, receives):
+        up = lambda: remote(
+            source_up, target_down, sends.at[0], receives.at[0], {"band": band - 1}
+        )
+        down = lambda: remote(
+            source_down, target_up, sends.at[1], receives.at[1], {"band": band + 1}
+        )
+
+        def start():
+            pl.when(band > 0)(lambda: up().start())
+            pl.when(band < bands - 1)(lambda: down().start())
+
+        def finish():
+            pl.when(band > 0)(lambda: down().wait_recv())
+            pl.when(band < bands - 1)(lambda: up().wait_recv())
+            pl.when(band > 0)(lambda: up().wait_send())
+            pl.when(band < bands - 1)(lambda: down().wait_send())
+
+        return start, finish
+
+    def input_sides(source, field, slot, place):
+        return sides(
+            source.at[:, pl.ds(0, 8)],
+            source.at[:, pl.ds(rows - 8, 8)],
+            states.at[field, slot, :, upper],
+            states.at[field, slot, :, lower],
+            send.at[field, place],
+            receive.at[field, place],
+        )
+
+    def state_sides(field, pair):
+        slot = 2 * pair + 1
+        return sides(
+            states.at[field, slot, :, pl.ds(lead, 8)],
+            states.at[field, slot, :, pl.ds(lead + rows - 8, 8)],
+            states.at[field, slot, :, upper],
+            states.at[field, slot, :, lower],
+            send.at[field, pair],
+            receive.at[field, pair],
+        )
+
+    opening = [
+        input_sides(wave_now, 0, 1, 0),
+        input_sides(wave_before, 0, 0, pairs),
+        sides(
+            velocity.at[pl.ds(0, 8)],
+            velocity.at[pl.ds(rows - 8, 8)],
+            speeds.at[upper],
+            speeds.at[lower],
+            speed_send,
+            speed_receive,
+        ),
+        input_sides(adjoint_last, 1, 1, 0),
+        input_sides(adjoint_after, 1, 0, pairs),
+    ]
+    for start, finish in opening:
+        start()
+
+    def near_copy(sender, target, peer):
+        return remote(
+            velocity,
+            near_speed.at[pl.ds(margin + sender * rows, rows)],
+            near_send.at[target],
+            near_receive.at[sender],
+            {"band": peer},
+        )
+
+    def each_near(action):
+        for sender in range(near_bands):
+            for target in range(near_bands):
+                if sender != target:
+                    action(sender, target)
+
+    each_near(lambda sender, target: pl.when(band == sender)(lambda: near_copy(sender, target, target).start()))
+
+    states[0, 1, :, own] = wave_now[...]
+    states[0, 0, :, own] = wave_before[...]
+    states[1, 1, :, own] = adjoint_last[...]
+    states[1, 0, :, own] = adjoint_after[...]
+    for start, finish in opening:
+        finish()
+    speeds[own] = velocity[...]
+    speeds[lead - 8 : lead + rows + 8] = (speeds[lead - 8 : lead + rows + 8] * speed_factor) ** 2
+
+    def grow(field, slot, first, last):
+        for shot in range(shots):
+            for row in range(first, last, 8):
+                states[field, slot + 1, shot, row : row + 8] = advance(
+                    lambda reach: states[field, slot, shot, row + reach : row + reach + 8],
+                    states[field, slot - 1, shot, row : row + 8],
+                    speeds[row : row + 8],
+                )
+            if field == 0:
+                spot = slice(lead + source_depth, lead + source_depth + 1)
+                states[0, slot + 1, shot, spot] = (
+                    states[0, slot + 1, shot, spot] + drive[slot - 1, shot : shot + 1]
+                )
+
+    def pair_step(pair, carry):
+        for field in range(2):
+            pl.when(pair > 0)(lambda: state_sides(field, pair)[1]())
+            grow(field, 2 * pair + 1, lead - 8, lead + rows + 8)
+            grow(field, 2 * pair + 2, lead, lead + rows)
+            pl.when(pair < pairs - 1)(lambda: state_sides(field, pair + 1)[0]())
+        return carry
+
+    lax.fori_loop(0, pairs, pair_step, 0)
+
+    @pl.when(band == 0)
+    def _():
+        spot = lead + receiver_depth
+        for step in range(steps):
+            for shot in range(shots):
+                injected[step, shot : shot + 1] = (
+                    states[0, step + 2, shot, spot : spot + 1] * marked[shot : shot + 1]
+                    - recorded[step, shot : shot + 1]
+                )
+
+    def burst_copy(target, peer):
+        return remote(
+            injected, injected, burst_send.at[target], burst_receive, {"band": peer}
+        )
+
+    for target in range(1, near_bands):
+        pl.when(band == 0)(lambda: burst_copy(target, target).start())
+    each_near(
+        lambda sender, target: pl.when(band == target)(
+            lambda: near_copy(sender, target, sender).wait_recv()
+        )
+    )
+    each_near(
+        lambda sender, target: pl.when(band == sender)(
+            lambda: near_copy(sender, target, target).wait_send()
+        )
+    )
+
+    @pl.when(band < near_bands)
+    def _():
+        start = pl.multiple_of(margin + band * rows, 8)
+        near_speed[pl.ds(start, rows)] = velocity[...]
+        near_speed[...] = (near_speed[...] * speed_factor) ** 2
+        bursts[...] = jnp.zeros(bursts.shape, jnp.float32)
+
+    for target in range(1, near_bands):
+        pl.when(band == target)(lambda: burst_copy(target, 0).wait_recv())
+        pl.when(band == 0)(lambda: burst_copy(target, target).wait_send())
+
+    @pl.when(band < near_bands)
+    def _():
+        def burst_step(index, carry):
+            now = index % 2
+            other = 1 - now
+            reached = (index + 2) // 2
+            needed = ((band + 1) * rows + 4 * (steps - 1 - index) + 7) // 8
+            blocks = lax.min(lax.min(reached, needed), near_bands * rows // 8)
+
+            def block(number, inner):
+                row = pl.multiple_of(margin + number * 8, 8)
+                for shot in range(shots):
+                    tile = bursts[now, shot, pl.ds(row - 8, 24)]
+                    bursts[other, shot, pl.ds(row, 8)] = advance(
+                        lambda reach: tile[8 + reach : 16 + reach],
+                        bursts[other, shot, pl.ds(row, 8)],
+                        near_speed[pl.ds(row, 8)],
+                        )
+                return inner
+
+            lax.fori_loop(0, blocks, block, 0)
+            spot = slice(margin + receiver_depth, margin + receiver_depth + 1)
+            start = pl.multiple_of(margin + band * rows, 8)
+            for shot in range(shots):
+                bursts[other, shot, spot] = (
+                    bursts[other, shot, spot] + injected[steps - 1 - index, shot : shot + 1]
+                )
+                states[1, index + 2, shot, own] = (
+                    states[1, index + 2, shot, own] + bursts[other, shot, pl.ds(start, rows)]
+                )
+            return carry
+
+        lax.fori_loop(0, steps, burst_step, 0)
+
+    for row in range(0, rows, 8):
+        def accumulate(index, running):
+            for shot in range(shots):
+                running = running + (
+                    states[0, steps + 1 - index, shot, lead + row : lead + row + 8]
+                    * states[1, index + 2, shot, lead + row : lead + row + 8]
+                )
+            return running
+
+        image[row : row + 8] = lax.fori_loop(
+            0, steps, accumulate, jnp.zeros((8, breadth), jnp.float32)
+        )
+
+
+def wave_image(
+    velocity, wave_now, wave_before, adjoint_last, adjoint_after, drive, marked, recorded
+):
+    shots, rows, breadth = wave_now.shape
+    steps = drive.shape[0]
+    bands = lax.axis_size("band")
+    reach = receiver_depth + 1 + 4 * (steps - 1)
+    near_bands = min(bands, -(-reach // rows))
+    f32 = jnp.float32
+    dma = pltpu.SemaphoreType.DMA
+    tall = rows + 2 * lead
+    return pl.pallas_call(
+        functools.partial(wave_kernel, bands, near_bands),
+        name="wave_image",
+        out_shape=jax.ShapeDtypeStruct((rows, breadth), f32),
+        in_specs=vmem(8),
+        out_specs=vmem(1)[0],
+        scratch_shapes=[
+            pltpu.VMEM((2, steps + 2, shots, tall, breadth), f32),
+            pltpu.VMEM((tall, breadth), f32),
+            pltpu.VMEM((near_bands * rows + 16, breadth), f32),
+            pltpu.VMEM((2, shots, near_bands * rows + 16, breadth), f32),
+            pltpu.VMEM((steps, shots, breadth), f32),
+            dma((2, steps // 2 + 1, 2)),
+            dma((2, steps // 2 + 1, 2)),
+            dma((2,)),
+            dma((2,)),
+            dma((near_bands,)),
+            dma((near_bands,)),
+            dma((near_bands,)),
+            dma,
+        ],
+        compiler_params=pltpu.CompilerParams(
+            collective_id=3, has_side_effects=True, vmem_limit_bytes=48 * 1024 * 1024
+        ),
+    )(velocity, wave_now, wave_before, adjoint_last, adjoint_after, drive, marked, recorded)
 
 
 def halves(values):
@@ -540,64 +809,20 @@
     conv_out,
     cotangent,
 ):
-    rows_here = velocity.shape[0]
     breadth = velocity.shape[1]
     shot_here = wave_now.shape[0]
     num_steps = wavelet.shape[1]
     slots = observed.shape[2]
-    piece_cols = cotangent.shape[1]
-    first_row = lax.axis_index("band") * rows_here
-    speed_sq = (velocity * speed_factor) ** 2
     columns = jnp.arange(breadth, dtype=jnp.int32)
-    source_cols = (columns[None, :] == source_col[:, None]).astype(jnp.float32)[:, None, :]
+    source_cols = (columns[None, :] == source_col[:, None]).astype(jnp.float32)
+    topmost = (lax.axis_index("band") == 0).astype(jnp.float32)
+    drive = wavelet.T[:, :, None] * (source_cols * topmost)[None]
     table = receiver_table(rec_first, rec_last, rec_count, breadth, slots)
-    active = (jnp.arange(slots, dtype=jnp.int32)[None, :] < rec_count[:, None]).astype(jnp.float32)
-
-    def source_term(row_start, height, amount):
-        row_ids = row_start + jnp.arange(height, dtype=jnp.int32)
-        marked = (row_ids == source_depth).astype(jnp.float32)[None, :, None]
-        return marked * source_cols * amount[:, None, None]
-
-    def receiver_term(row_start, height, residual):
-        row_ids = row_start + jnp.arange(height, dtype=jnp.int32)
-        marked = (row_ids == receiver_depth).astype(jnp.float32)[None, :, None]
-        injected = jnp.einsum("swk,sk->sw", table, residual, precision=highest)
-        return marked * injected[:, None, :]
-
-    speed_wide = extended_2(speed_sq, (("band", 0),), 16)
-
-    def propagate(start, prior, drive, inject):
-        grouped = drive.reshape((num_steps // 4, 4) + drive.shape[1:])
-
-        def block(carry, amounts):
-            stacked = extended_2(jnp.stack([carry[0], carry[1]]), (("band", 2),), 16)
-            current = stacked[0]
-            earlier = stacked[1]
-            margin = 16
-            saved = []
-            for offset in range(4):
-                inner = margin - 4
-                speed_part = speed_wide[16 - inner : 16 + rows_here + inner]
-                fresh = (
-                    2.0 * current[:, 4:-4]
-                    - earlier[:, 4:-4]
-                    + speed_part * laplace(current)
-                    + inject(first_row - inner, rows_here + 2 * inner, amounts[offset])
-                )
-                earlier = current[:, 4:-4]
-                current = fresh
-                margin = inner
-                saved.append(fresh[:, inner : inner + rows_here])
-            return ((current, earlier), jnp.stack(saved))
-
-        ignored, states = lax.scan(block, (start, prior), grouped)
-        return states.reshape((num_steps,) + start.shape)
-
-    stored = propagate(wave_now, wave_before, wavelet.T, source_term)
-    samples = jnp.einsum("tsw,swk->tsk", stored[:, :, receiver_depth, :], table, precision=highest)
-    misfit = (samples - jnp.transpose(observed, (1, 0, 2))) * active[None]
-    adjoint = propagate(adjoint_last, adjoint_after, misfit[::-1], receiver_term)
-    imaging = jnp.sum(stored * adjoint[::-1], axis=(0, 1))
+    marked = jnp.sum(table, axis=2)
+    recorded = jnp.einsum("stk,swk->tsw", observed, table, precision=highest)
+    imaging = wave_image(
+        velocity, wave_now, wave_before, adjoint_last, adjoint_after, drive, marked, recorded
+    )
     group_count = shot_here * lax.axis_size(("shot", "net"))
     return update_model(
         imaging, velocity, cotangent, num_steps, group_count, conv_in, conv_mid, conv_out

time: 226 us -> 141 us (0.62)
  Pallas kernels: 47.4 us -> 124 us
  starting transfers between devices: 55.6 us -> 0 us
  other arithmetic: 49.7 us -> 1.77 us
  local copies, waits for them, and re-layouts: 36.7 us -> 12.5 us
  matrix products: 17.3 us -> 0.61 us
  waiting for transfers between devices: 15.9 us -> 0 us
    pallas_call x0 -> x1, Pallas kernels: none -> 74.4 us  [wave_image(): pl.pallas_call(functools.partial(wave_kernel, bands, near_bands), name='w...]
    ppermute x18 -> x0, starting transfers between devices: 55.6 us -> none  [the longest x9 44 us: extended_2(): lax.ppermute(lax.slice_in_dim(block, block.shape[dim] - width, None, axis...]
    add x24 -> x0, other arithmetic: 21.6 us -> none  [block(): 2.0 * current[:, 4:-4] - earlier[:, 4:-4] + speed_part * laplace(current)]
    dot_general x17 -> x1, matrix products: 17.3 us -> 0.61 us  [on_device(): recorded = jnp.einsum('stk,swk->tsw', observed, table, precision=highest)]
    ppermute x18 -> x0, waiting for transfers between devices: 15.9 us -> none  [the longest x9 10.6 us: extended_2(): lax.ppermute(lax.slice_in_dim(block, 0, width, axis=dim), axis, backward)]
    reshape x2 -> x0, local copies, waits for them, and re-layouts: 11.2 us -> none  [propagate(): return states.reshape((num_steps,) + start.shape)]
    dynamic_update_slice x8 -> x0, other arithmetic: 8.83 us -> none  [propagate(): ignored, states = lax.scan(block, (start, prior), grouped)]
    rev x2 -> x0, local copies, waits for them, and re-layouts: 6.72 us -> none  [the longest x1 6.71 us: on_device(): imaging = jnp.sum(stored * adjoint[::-1], axis=(0, 1))]
  transfers between devices with their start and end apart: 18 -> 0, of which waited for: 8 -> 0; matrix products, arithmetic and copies ran while one was open for 11% -> 0% of each run, Pallas kernels for 0% -> 0%
where the time goes in v2:
time: 141 us; the launch traced here: 140 us
  Pallas kernels  124 us (88%)
  local copies, waits for them, and re-layouts  12.5 us (9%)
  other arithmetic  1.77 us (1%)
    pallas_call x1, Pallas kernels, wave_image(): pl.pallas_call(functools.partial(wave_kernel, bands, near_bands), name='w...  74.4 us
    pallas_call x1, Pallas kernels, gather_pieces(): pl.pallas_call(functools.partial(gather_kernel, groups, nets, bands), nam...  18 us
    pallas_call x1, Pallas kernels, total_grads(): pl.pallas_call(functools.partial(total_kernel, sizes), name='total_grads'...  16.3 us
    pallas_call x1, Pallas kernels, network(): pl.pallas_call(functools.partial(network_kernel, width), name='network',...  15.6 us
    unnamed x47, local copies, waits for them, and re-layouts  5.97 us

profile of v2, /device:TPU:0, one launch (start us, length us, event | category | flops | bytes accessed | tf_op | source)
XLA Modules:
  0.0 140.3 jit_solution(15616962234690696881)
XLA Ops:
  0.6 0.0 copy-start
  0.6 0.7 reduce
  1.4 0.1 reshape.208
  1.5 0.0 copy-start.15
  1.5 0.1 copy.29
  1.6 0.6 copy-done.15
  2.2 0.0 copy-start.8
  2.2 0.1 copy.28
  2.3 0.7 copy-done.8
  3.0 0.1 copy.30
  3.1 0.0 copy-start.18
  3.1 0.1 copy.31
  3.3 0.0 copy-start.7
  3.3 0.1 copy.34.middle_back
  3.4 0.1 reshape.212
  3.4 0.3 copy-done.18
  3.8 0.1 compare_select_fusion
  3.9 0.7 copy-done.17
  4.6 0.1 copy.32
  4.6 0.1 broadcast_multiply_fusion.drive
  4.7 0.0 copy-done.21
  4.8 0.0 copy-done.19
  4.8 0.2 fusion.13
  5.0 0.1 iota_compare_fusion.1
  5.1 0.4 convert_reduce_fusion.marked
  5.4 0.0 copy-start.4
  5.5 0.0 copy-start.5
  5.5 0.6 fusion.1
  6.1 0.1 copy.41
  6.2 0.2 copy-done.4
  6.4 0.1 copy-done.5
  6.5 0.5 copy-done.1
  7.0 74.4 %wave_image.1.image = f32[32,1024]{1,0:T(8,128)S(1)} custom-call(f32[32,1024]{1,0:T(8,128)S(1)} %copy-done.1, f32[2,32,1024]{2,1,0:T(8,128)S(1)} %copy-done.4, f32[2,32,1024]{2,1,0:T(8,128)S(1)} %copy-done.5, f32[2,32,1024]{2,1,0:T(8,128)S(1)} %copy-done.6, f32[2,32,1024]{2,1,0:T(8,128)S(1)} %copy-done.7, f32[16,2,1024]{2,1,0:T(2,128)S(1)} %broadcast_multiply_fusion.drive, ...), custom_call_target="tpu_custom_call" | custom-call | tf_op jit(solution)/shard_map/wave_image/pallas_call | solution.py:591
  81.5 0.7 copy-done.3
  82.2 18.0 %gather_pieces.1 = (f32[48,384]{1,0:T(8,128)}, f32[48,384]{1,0:T(8,128)}, f32[8,1024]{1,0:T(8,128)}, f32[8,1024]{1,0:T(8,128)}) custom-call(f32[32,1024]{1,0:T(8,128)} %copy-done.3, f32[32,1024]{1,0:T(8,128)} %velocity.3, f32[32,128]{1,0:T(8,128)} %cotangent.1), custom_call_target="tpu_custom_call" | custom-call | tf_op jit(solution)/shard_map/gather_pieces/pallas_call | solution.py:195
  100.2 0.8 slice.36
  101.0 0.1 fusion.7
  101.1 0.0 copy-start.11
  101.1 0.2 stack.22
  101.3 0.6 copy-done.12
  101.9 0.0 copy-done.13
  101.9 0.1 slice_multiply_fusion.1
  102.0 0.2 stack.23
  102.2 0.2 stack.24
  102.4 0.2 stack.25
  102.6 0.1 and.62
  102.6 0.2 and.63
  102.8 0.2 and.66
  103.1 0.0 copy-start.14
  103.1 0.7 copy-done.14
  103.8 0.2 stack.28
  104.0 15.6 %network.1 = (f32[1,5120]{1,0:T(1,128)S(1)}, f32[32,640]{1,0:T(8,128)S(1)}) custom-call(f32[64,72]{1,0:T(8,128)S(1)} %pad_maximum_fusion.first, f32[32,288]{1,0:T(8,128)S(1)} %copy-done.8, f32[32,288]{1,0:T(8,128)S(1)} %copy.34.middle_back, f32[16,32]{1,0:T(8,128)S(1)} %pad.22.last, f32[8,5120]{1,0:T(8,128)S(1)} %pad.24.layers), custom_call_target="tpu_custom_call" | custom-call | tf_op jit(solution)/shard_map/network/pallas_call | solution.py:736
  119.6 0.0 copy-start.9
  119.6 0.6 copy-done.9
  120.3 0.1 slice_reduce_fusion
  120.3 0.1 reshape_squeeze.3
  120.5 0.7 slice.48
  121.2 16.3 %total_grads.1 = f32[32,640]{1,0:T(8,128)} custom-call(f32[32,640]{1,0:T(8,128)} %copy-done.9), custom_call_target="tpu_custom_call" | custom-call | tf_op jit(solution)/shard_map/total_grads/pallas_call | solution.py:298
  137.5 0.8 fusion.15
  138.3 0.1 copy.35
  138.3 0.6 reshape.214
  139.0 0.6 slice.45
  139.6 0.1 copy.36
  139.7 0.6 reshape.216
  (41 shorter events, 0.3 us)
Async XLA Ops:
  0.6 4.8 %copy-start = (f32[2,16,128]{2,1,0:T(8,128)S(1)}, f32[2,16,128]{2,1,0:T(8,128)}, u32[]{:S(2)}) copy-start(f32[2,16,128]{2,1,0:T(8,128)} %param.26) | copy-start | bytes 49156
  1.5 0.7 copy-start.15
  2.2 0.8 copy-start.8
  3.1 0.7 copy-start.18
  3.3 2.9 %copy-start.7 = (f32[2,32,1024]{2,1,0:T(8,128)S(1)}, f32[2,32,1024]{2,1,0:T(8,128)}, u32[]{:S(2)}) copy-start(f32[2,32,1024]{2,1,0:T(8,128)} %adjoint_after.1) | copy-start | bytes 786436
  3.8 1.0 copy-start.21
  3.8 1.0 copy-start.19
  3.8 1.0 copy-start.20
  3.9 0.7 copy-start.17
  4.6 1.6 %copy-start.6 = (f32[2,32,1024]{2,1,0:T(8,128)S(1)}, f32[2,32,1024]{2,1,0:T(8,128)}, u32[]{:S(2)}) copy-start(f32[2,32,1024]{2,1,0:T(8,128)} %adjoint_last.1) | copy-start | bytes 786436
  5.4 1.0 copy-start.4
  5.5 1.0 copy-start.5
  6.1 1.0 copy-start.1
  81.5 0.7 copy-start.3
  82.2 18.8 %copy-start.2 = (f32[32,1024]{1,0:T(8,128)S(1)}, f32[32,1024]{1,0:T(8,128)}, u32[]{:S(2)}) copy-start(f32[32,1024]{1,0:T(8,128)} %velocity.3) | copy-start | bytes 393220
  100.2 0.8 copy-start.16
  101.0 0.9 copy-start.12
  101.0 0.9 copy-start.13
  101.1 0.8 copy-start.11
  103.1 0.7 copy-start.14
  119.6 0.6 copy-start.9
  137.5 1.5 %copy-start.10 = (f32[32,640]{1,0:T(8,128)S(1)}, f32[32,640]{1,0:T(8,128)}, u32[]{:S(2)}) copy-start(f32[32,640]{1,0:T(8,128)} %total_grads.1) | copy-start | bytes 245764

commit v3 on v2

--- a/solution.py
+++ b/solution.py
@@ -59,7 +59,7 @@
 def gather_kernel(
     groups, nets, bands, image, velocity, cotangent,
     out_image, out_cot, out_low, out_high,
-    padded, slots, total, halo, speed_halo,
+    packed, slots, total, halo, speed_halo,
     send, receive, side_send, side_receive, row_send, row_receive,
 ):
     rows, breadth = image.shape
@@ -89,18 +89,22 @@
     def _():
         pl.semaphore_signal(barrier, inc=1, device_id={"band": band + 1}, device_id_type=MESH)
 
-    padded[:, :piece] = jnp.zeros((rows, piece), jnp.float32)
-    padded[:, piece + breadth :] = jnp.zeros((rows, piece), jnp.float32)
-    padded[:, piece : piece + breadth] = image[...]
+    left_half = lax.broadcasted_iota(jnp.int32, (rows, piece), 1) < piece // 2
+    blank = jnp.zeros((rows, piece), jnp.float32)
+    for index in range(groups):
+        first = index * piece
+        before = image[:, first - piece : first] if index > 0 else blank
+        after = image[:, first + piece : first + 2 * piece] if index < groups - 1 else blank
+        packed[index, :, :piece] = image[:, first : first + piece]
+        packed[index, :, piece:] = jnp.where(left_half, after, before)
     pl.semaphore_wait(
         barrier, groups - 1 + lax.min(band, 1) + lax.min(bands - 1 - band, 1)
     )
 
     def scatter(step):
         target = lax.rem(me + step, groups)
-        start = pl.multiple_of(target * piece, 128)
         return remote(
-            padded.at[:, pl.ds(start, 3 * piece)],
+            packed.at[target],
             slots.at[step],
             send.at[step],
             receive.at[step],
@@ -151,14 +155,15 @@
     pl.when(band > 0)(lambda: speed_up().start())
     pl.when(band < bands - 1)(lambda: speed_down().start())
 
-    own = pl.multiple_of(me * piece, 128)
-    slots[0] = padded[:, pl.ds(own, 3 * piece)]
+    slots[0] = packed[me]
     for step in range(1, groups):
         scatter(step).wait_recv()
     summed = slots[0]
     for step in range(1, groups):
         summed = summed + slots[step]
-    total[0] = summed
+    total[0, :, :piece] = summed[:, piece:]
+    total[0, :, piece : 2 * piece] = summed[:, :piece]
+    total[0, :, 2 * piece :] = summed[:, piece:]
     pl.when(me > 0)(lambda: to_right().wait_recv())
     pl.when(me < groups - 1)(lambda: to_left().wait_recv())
     total[1, :, piece : 2 * piece] = cotangent[...]
@@ -200,8 +205,8 @@
         in_specs=vmem(3),
         out_specs=vmem(4),
         scratch_shapes=[
-            pltpu.VMEM((rows, breadth + 2 * piece), f32),
-            pltpu.VMEM((groups, rows, 3 * piece), f32),
+            pltpu.VMEM((groups, rows, 2 * piece), f32),
+            pltpu.VMEM((groups, rows, 2 * piece), f32),
             pltpu.VMEM((2, rows, 3 * piece), f32),
             pltpu.VMEM((2, 2, 8, 3 * piece), f32),
             pltpu.VMEM((2, 8, breadth), f32),
@@ -466,15 +471,19 @@
     speeds[own] = velocity[...]
     speeds[lead - 8 : lead + rows + 8] = (speeds[lead - 8 : lead + rows + 8] * speed_factor) ** 2
 
-    def grow(field, slot, first, last):
+    inner = list(range(lead + 8, lead + rows - 8, 8))
+    edges = [row for row in range(lead, lead + rows, 8) if row not in inner]
+    outer = [lead - 8] + edges + [lead + rows]
+
+    def grow(field, slot, chosen):
         for shot in range(shots):
-            for row in range(first, last, 8):
+            for row in chosen:
                 states[field, slot + 1, shot, row : row + 8] = advance(
                     lambda reach: states[field, slot, shot, row + reach : row + reach + 8],
                     states[field, slot - 1, shot, row : row + 8],
                     speeds[row : row + 8],
                 )
-            if field == 0:
+            if field == 0 and lead in chosen:
                 spot = slice(lead + source_depth, lead + source_depth + 1)
                 states[0, slot + 1, shot, spot] = (
                     states[0, slot + 1, shot, spot] + drive[slot - 1, shot : shot + 1]
@@ -482,10 +491,12 @@
 
     def pair_step(pair, carry):
         for field in range(2):
+            grow(field, 2 * pair + 1, inner)
             pl.when(pair > 0)(lambda: state_sides(field, pair)[1]())
-            grow(field, 2 * pair + 1, lead - 8, lead + rows + 8)
-            grow(field, 2 * pair + 2, lead, lead + rows)
+            grow(field, 2 * pair + 1, outer)
+            grow(field, 2 * pair + 2, edges)
             pl.when(pair < pairs - 1)(lambda: state_sides(field, pair + 1)[0]())
+            grow(field, 2 * pair + 2, inner)
         return carry
 
     lax.fori_loop(0, pairs, pair_step, 0)

time: 141 us -> 136 us (0.965)
  Pallas kernels: 124 us -> 119 us
    pallas_call x1, Pallas kernels: 74.4 us -> 70.5 us  [wave_image(): pl.pallas_call(functools.partial(wave_kernel, bands, near_bands), name='w...]
where the time goes in v3:
time: 136 us; the launch traced here: 135 us
  Pallas kernels  119 us (88%)
  local copies, waits for them, and re-layouts  12.5 us (9%)
  other arithmetic  1.77 us (1%)
    pallas_call x1, Pallas kernels, wave_image(): pl.pallas_call(functools.partial(wave_kernel, bands, near_bands), name='w...  70.5 us
    pallas_call x1, Pallas kernels, gather_pieces(): pl.pallas_call(functools.partial(gather_kernel, groups, nets, bands), nam...  16.6 us
    pallas_call x1, Pallas kernels, total_grads(): pl.pallas_call(functools.partial(total_kernel, sizes), name='total_grads'...  16.4 us
    pallas_call x1, Pallas kernels, network(): pl.pallas_call(functools.partial(network_kernel, width), name='network',...  15.5 us
    unnamed x47, local copies, waits for them, and re-layouts  5.97 us

profile of v3, /device:TPU:0, one launch (start us, length us, event | category | flops | bytes accessed | tf_op | source)
XLA Modules:
  0.0 135.1 jit_solution(13032463825794541792)
XLA Ops:
  0.6 0.0 copy-start
  0.6 0.7 reduce
  1.4 0.1 reshape.208
  1.5 0.0 copy-start.15
  1.5 0.1 copy.29
  1.6 0.6 copy-done.15
  2.2 0.0 copy-start.8
  2.2 0.1 copy.28
  2.3 0.7 copy-done.8
  3.0 0.1 copy.30
  3.1 0.0 copy-start.18
  3.1 0.1 copy.31
  3.3 0.0 copy-start.7
  3.3 0.1 copy.34.middle_back
  3.4 0.1 reshape.212
  3.4 0.3 copy-done.18
  3.8 0.1 compare_select_fusion
  3.9 0.7 copy-done.17
  4.6 0.1 copy.32
  4.6 0.1 broadcast_multiply_fusion.drive
  4.7 0.0 copy-done.21
  4.8 0.2 fusion.13
  5.0 0.1 iota_compare_fusion.1
  5.1 0.4 convert_reduce_fusion.marked
  5.4 0.0 copy-start.4
  5.5 0.0 copy-start.5
  5.5 0.6 fusion.1
  6.1 0.1 copy.41
  6.2 0.0 copy-done.7
  6.2 0.0 copy-done.6
  6.2 0.2 copy-done.4
  6.4 0.1 copy-done.5
  6.5 0.5 copy-done.1
  7.0 70.5 %wave_image.1.image = f32[32,1024]{1,0:T(8,128)S(1)} custom-call(f32[32,1024]{1,0:T(8,128)S(1)} %copy-done.1, f32[2,32,1024]{2,1,0:T(8,128)S(1)} %copy-done.4, f32[2,32,1024]{2,1,0:T(8,128)S(1)} %copy-done.5, f32[2,32,1024]{2,1,0:T(8,128)S(1)} %copy-done.6, f32[2,32,1024]{2,1,0:T(8,128)S(1)} %copy-done.7, f32[16,2,1024]{2,1,0:T(2,128)S(1)} %broadcast_multiply_fusion.drive, ...), custom_call_target="tpu_custom_call" | custom-call | tf_op jit(solution)/shard_map/wave_image/pallas_call | solution.py:602
  77.6 0.7 copy-done.3
  78.2 16.6 %gather_pieces.1 = (f32[48,384]{1,0:T(8,128)}, f32[48,384]{1,0:T(8,128)}, f32[8,1024]{1,0:T(8,128)}, f32[8,1024]{1,0:T(8,128)}) custom-call(f32[32,1024]{1,0:T(8,128)} %copy-done.3, f32[32,1024]{1,0:T(8,128)} %velocity.3, f32[32,128]{1,0:T(8,128)} %cotangent.1), custom_call_target="tpu_custom_call" | custom-call | tf_op jit(solution)/shard_map/gather_pieces/pallas_call | solution.py:200
  94.9 0.8 slice.36
  95.7 0.1 fusion.7
  95.8 0.0 copy-start.11
  95.8 0.2 stack.22
  96.0 0.6 copy-done.12
  96.6 0.0 copy-done.13
  96.6 0.1 slice_multiply_fusion.1
  96.7 0.2 stack.23
  96.9 0.2 stack.24
  97.0 0.2 stack.25
  97.2 0.1 and.62
  97.3 0.2 and.63
  97.5 0.2 and.66
  97.7 0.0 copy-start.14
  97.8 0.7 copy-done.14
  98.5 0.2 stack.28
  98.7 15.5 %network.1 = (f32[1,5120]{1,0:T(1,128)S(1)}, f32[32,640]{1,0:T(8,128)S(1)}) custom-call(f32[64,72]{1,0:T(8,128)S(1)} %pad_maximum_fusion.first, f32[32,288]{1,0:T(8,128)S(1)} %copy-done.8, f32[32,288]{1,0:T(8,128)S(1)} %copy.34.middle_back, f32[16,32]{1,0:T(8,128)S(1)} %pad.22.last, f32[8,5120]{1,0:T(8,128)S(1)} %pad.24.layers), custom_call_target="tpu_custom_call" | custom-call | tf_op jit(solution)/shard_map/network/pallas_call | solution.py:747
  114.3 0.6 copy-done.9
  114.9 0.1 slice_reduce_fusion
  115.0 0.1 reshape_squeeze.3
  115.1 0.7 slice.48
  115.8 16.4 %total_grads.1 = f32[32,640]{1,0:T(8,128)} custom-call(f32[32,640]{1,0:T(8,128)} %copy-done.9), custom_call_target="tpu_custom_call" | custom-call | tf_op jit(solution)/shard_map/total_grads/pallas_call | solution.py:303
  132.2 0.8 fusion.15
  133.0 0.1 copy.35
  133.1 0.6 reshape.214
  133.7 0.6 slice.45
  134.3 0.1 copy.36
  134.4 0.6 reshape.216
  (41 shorter events, 0.3 us)
Async XLA Ops:
  0.6 4.8 %copy-start = (f32[2,16,128]{2,1,0:T(8,128)S(1)}, f32[2,16,128]{2,1,0:T(8,128)}, u32[]{:S(2)}) copy-start(f32[2,16,128]{2,1,0:T(8,128)} %param.26) | copy-start | bytes 49156
  1.5 0.7 copy-start.15
  2.2 0.8 copy-start.8
  3.1 0.7 copy-start.18
  3.3 2.9 %copy-start.7 = (f32[2,32,1024]{2,1,0:T(8,128)S(1)}, f32[2,32,1024]{2,1,0:T(8,128)}, u32[]{:S(2)}) copy-start(f32[2,32,1024]{2,1,0:T(8,128)} %adjoint_after.1) | copy-start | bytes 786436
  3.8 1.0 copy-start.21
  3.8 1.0 copy-start.19
  3.8 1.0 copy-start.20
  3.9 0.7 copy-start.17
  4.6 1.6 %copy-start.6 = (f32[2,32,1024]{2,1,0:T(8,128)S(1)}, f32[2,32,1024]{2,1,0:T(8,128)}, u32[]{:S(2)}) copy-start(f32[2,32,1024]{2,1,0:T(8,128)} %adjoint_last.1) | copy-start | bytes 786436
  5.4 1.0 copy-start.4
  5.5 1.0 copy-start.5
  6.1 1.0 copy-start.1
  77.6 0.7 copy-start.3
  78.2 17.4 %copy-start.2 = (f32[32,1024]{1,0:T(8,128)S(1)}, f32[32,1024]{1,0:T(8,128)}, u32[]{:S(2)}) copy-start(f32[32,1024]{1,0:T(8,128)} %velocity.3) | copy-start | bytes 393220
  94.9 0.8 copy-start.16
  95.7 0.9 copy-start.12
  95.7 0.9 copy-start.13
  95.8 0.8 copy-start.11
  97.7 0.7 copy-start.14
  114.3 0.6 copy-start.9
  132.2 1.5 %copy-start.10 = (f32[32,640]{1,0:T(8,128)S(1)}, f32[32,640]{1,0:T(8,128)}, u32[]{:S(2)}) copy-start(f32[32,640]{1,0:T(8,128)} %total_grads.1) | copy-start | bytes 245764
